TPU v7x, 128 devices: a whole 4x4x4 slice. The times are simulated.
128 devices in a mesh: lat: 8 (over z, core), lon: 16 (over x, y).
Axes of the slice: x: 4, y: 4, z: 4, core: 2. Of those that a mesh axis runs over, the one named last changes fastest.
Arguments:
- adjoint_state: float32 [2, 72, 128, 2048], P(None, None, 'lat', 'lon'), may hold values from -6 to 6
- courant_east: float32 [72, 128, 2048], P(None, 'lat', 'lon'), may hold values from -0.45 to 0.45
- courant_north: float32 [72, 128, 2048], P(None, 'lat', 'lon'), may hold values from -0.45 to 0.45
- diffusion: float32 [128, 2048], P('lat', 'lon'), may hold values from 0.05 to 0.45
- convective_flux: float32 [128, 2048], P('lat', 'lon'), may hold values from 0.1 to 1
- convection: float32 [72, 72], replicated, may hold values from -0.75 to 0.75
- sounding_forcing: bfloat16 [786432, 128], P(('lat', 'lon')), may hold values from -6 to 6
- sounding_column: int32 [786432], P(('lat', 'lon')), may hold values from 0 to 2047
- sounding_level: int32 [786432], P(('lat', 'lon')), may hold values from 0 to 8
- owner_counts: int32 [128, 128], P(('lat', 'lon')), may hold values from 8 to 48, as said below
Outputs:
- adjoint_final: float32 [2, 72, 128, 2048], P(None, None, 'lat', 'lon')
- flux_gradient: float32 [2, 128, 2048], P(None, 'lat', 'lon')
Inputs may be any that keep to these rules, and one draw needn't show every extreme that they name: `owner_counts`: each owner gets max(1, 8) to 48 rows of every device's list; every device sends exactly 48 to one owner, the same owner for all devices; the blocks stand in order of owner from row 0, and rows past the device's total are unused.
All inputs are finite; a program needn't handle non-finite values.
Results may differ from a plain program's by a relative error of at most 0.0003.
Values may be sent and summed in bfloat16 or wider, within the bound.
A program may use at most 64 MiB of HBM per device.

v0:
```python
import jax
import jax.numpy as jnp
from jax import lax
from jax.sharding import PartitionSpec as P

TR = 2
LEV = 72
SPAN = 64
CAP = 48


def passed_along(value, axis, steps):
    count = lax.axis_size(axis)
    pairs = [(source, (source + steps) % count) for source in range(count)]
    return lax.ppermute(value, axis, pairs)


def shifted(value, axis, by):
    peers = lax.axis_size(axis)
    pairs = [(i, i + by) for i in range(peers) if 0 <= i + by < peers]
    return lax.ppermute(value, axis, pairs)


def padded_2(value, sides, width):
    edges = {}
    for axis, dim in sides:
        peers, length = (lax.axis_size(axis), value.shape[dim])
        up = [(i, (i + 1) % peers) for i in range(peers)]
        last = lax.slice_in_dim(value, length - width, length, axis=dim)
        first = lax.slice_in_dim(value, 0, width, axis=dim)
        edges[dim] = (
            lax.ppermute(last, axis, up),
            lax.ppermute(first, axis, [(b, a) for a, b in up]),
        )
    done = []
    for _, dim in sides:
        low, high = edges[dim]
        around = [(width, width) if d in done else (0, 0) for d in range(value.ndim)]
        value = jnp.concatenate([jnp.pad(low, around), value, jnp.pad(high, around)], axis=dim)
        done.append(dim)
    return value


def column_physics(state, convection, diffusion, convective_flux):
    tracers, levels_n, lat_rows, lon_cols = state.shape
    flat = state.reshape(tracers, levels_n, lat_rows * lon_cols)
    mixed = jnp.einsum("lk,tlc->tkc", convection, flat, precision=lax.Precision.HIGHEST)
    mixed = flat + convective_flux.reshape(1, 1, -1) * mixed
    above = jnp.concatenate([mixed[:, 1:], mixed[:, -1:]], axis=1)
    below = jnp.concatenate([mixed[:, :1], mixed[:, :-1]], axis=1)
    mixed = mixed + diffusion.reshape(1, 1, -1) * (above - 2.0 * mixed + below)
    return mixed.reshape(tracers, levels_n, lat_rows, lon_cols)


def local(
    adjoint_state,
    courant_east,
    courant_north,
    diffusion,
    convective_flux,
    convection,
    sounding_forcing,
    sounding_column,
    sounding_level,
    owner_counts,
):
    lat_rows, lon_cols = diffusion.shape
    cells = lat_rows * lon_cols
    lat_size = lax.axis_size("lat")
    lon_size = lax.axis_size("lon")
    west_edge = passed_along(courant_east[:, :, -1:], "lon", 1)
    west_face = jnp.concatenate([west_edge, courant_east[:, :, :-1]], axis=2)
    south_edge = shifted(courant_north[:, -1:, :], "lat", 1)
    south_face = jnp.concatenate([south_edge, courant_north[:, :-1, :]], axis=1)
    top_band = lax.axis_index("lat") == lat_size - 1
    last_row = jnp.arange(lat_rows)[None, :, None] == lat_rows - 1
    north_face = jnp.where(last_row & top_band, 0.0, courant_north)
    east_gain = jnp.maximum(courant_east, 0.0)
    west_gain = jnp.minimum(west_face, 0.0)
    north_gain = jnp.maximum(north_face, 0.0)
    south_gain = jnp.minimum(south_face, 0.0)

    def advect(field):
        padded = padded_2(field, (("lat", 2), ("lon", 3)), 1)
        center = padded[:, :, 1:-1, 1:-1]
        east = padded[:, :, 1:-1, 2:]
        west = padded[:, :, 1:-1, :-2]
        north = padded[:, :, 2:, 1:-1]
        south = padded[:, :, :-2, 1:-1]
        result = center + east_gain * (east - center) + west_gain * (center - west)
        return result + north_gain * (north - center) + south_gain * (center - south)

    first = advect(column_physics(adjoint_state, convection, diffusion, convective_flux))
    row_counts = owner_counts[0]
    starts = jnp.cumsum(row_counts) - row_counts
    slot_ids = jnp.arange(CAP, dtype=jnp.int32)
    valid = slot_ids[None, :] < row_counts[:, None]
    row_ids = jnp.where(valid, starts[:, None] + slot_ids[None, :], 0)
    blocks = jnp.where(valid[:, :, None], sounding_forcing[row_ids], jnp.zeros((), jnp.bfloat16))
    codes = jnp.where(valid, sounding_level[row_ids] * cells + sounding_column[row_ids], -1)
    got_blocks, got_codes = (
        lax.all_to_all(blocks, ("lat", "lon"), split_axis=0, concat_axis=0, tiled=True),
        lax.all_to_all(codes, ("lat", "lon"), split_axis=0, concat_axis=0, tiled=True),
    )
    group_rows = lon_size * CAP
    got_blocks = got_blocks.reshape(lat_size, group_rows, TR, SPAN)
    got_codes = got_codes.reshape(lat_size, group_rows)
    cell_ids = jnp.arange(cells, dtype=jnp.int32)

    def place_group(total, items):
        group_blocks, group_codes = items
        received = group_codes >= 0
        levels = jnp.where(received, group_codes // cells, -1)
        columns = jnp.where(received, group_codes % cells, -1)
        arranged = jnp.transpose(group_blocks, (1, 2, 0))
        placed = jnp.zeros((TR, LEV, group_rows), jnp.bfloat16)
        for shift_level in range(LEV - SPAN + 1):
            moved = jnp.pad(arranged, ((0, 0), (shift_level, LEV - SPAN - shift_level), (0, 0)))
            placed = jnp.where((levels == shift_level)[None, None, :], moved, placed)
        selector = (columns[:, None] == cell_ids[None, :]).astype(jnp.bfloat16)
        added = jnp.dot(
            placed.reshape(TR * LEV, group_rows), selector, preferred_element_type=jnp.float32
        )
        return (total + added, None)

    forcing, unused = lax.scan(
        place_group, jnp.zeros((TR * LEV, cells), jnp.float32), (got_blocks, got_codes)
    )
    forced = first + forcing.reshape(TR, LEV, lat_rows, lon_cols)
    second = advect(column_physics(forced, convection, diffusion, convective_flux))
    return (second, forced[:, 0] + second[:, 0])


def solution(mesh):
    return jax.shard_map(
        local,
        mesh=mesh,
        in_specs=(
            P(None, None, "lat", "lon"),
            P(None, "lat", "lon"),
            P(None, "lat", "lon"),
            P("lat", "lon"),
            P("lat", "lon"),
            P(),
            P(("lat", "lon"), None),
            P(("lat", "lon")),
            P(("lat", "lon")),
            P(("lat", "lon"), None),
        ),
        out_specs=(P(None, None, "lat", "lon"), P(None, "lat", "lon")),
        check_vma=False,
    )
```

profile of v0, /device:TPU:0, one launch (start us, length us, event | category | flops | bytes accessed | tf_op | source)
XLA Modules:
  0.0 256.3 jit_solution(2656108707837715236)
XLA Ops:
  0.7 0.9 copy.52
  2.5 0.8 compare_select_fusion
  3.4 34.3 %gather_fusion = s32[6144]{0:T(1024)S(1)} fusion(s32[6144]{0:T(1024)S(1)} %copy-done.1, s32[6144]{0:T(1024)S(1)} %broadcast_clamp_fusion), kind=kCustom, calls=%fused_computation | custom fusion | bytes 73728 | tf_op jit(solution)/shard_map/gather | solution.py:100
  37.7 34.3 %gather_fusion.1 = s32[6144]{0:T(1024)S(1)} fusion(s32[6144]{0:T(1024)S(1)} %copy-done.2, s32[6144]{0:T(1024)S(1)} %broadcast_clamp_fusion), kind=kCustom, calls=%fused_computation.1 | custom fusion | bytes 73728 | tf_op jit(solution)/shard_map/gather | solution.py:100
  72.8 11.1 %all-to-all-start = ((s32[128,1,48]{2,1,0:T(1,128)}), s32[128,1,48]{2,1,0:T(1,128)S(1)}, u32[]{:S(2)}, u32[]{:S(2)}) async-start(s32[128,1,48]{2,1,0:T(1,128)} %bitcast.6), calls=%async_computation | async-start | bytes 131072 | tf_op jit(solution)/shard_map/all_to_all | solution.py:103
  84.0 2.4 reshape.513
  86.4 2.9 %fusion.12 = f32[2,72,2048]{2,1,0:T(8,128)S(1)} fusion(f32[2,72,2048]{2,1,0:T(8,128)} %reshape.513, f32[2048]{0:T(1024)S(1)} %bitcast.72, f32[72,72]{1,0:T(8,128)S(1)} %copy-done.10), kind=kOutput, calls=%fused_computation.36 | convolution fusion | flops 255393792 | bytes 2388224 | tf_op jit(solution)/shard_map/lk,tlc->tkc/dot_general | solution.py:47
  89.2 1.6 fusion.59
  91.0 22.1 %gather_fusion.2 = bf16[6144,128]{1,0:T(8,128)(2,1)} fusion(bf16[6144,128]{1,0:T(8,128)(2,1)S(1)} %copy-done, s32[6144]{0:T(1024)S(1)} %broadcast_clamp_fusion), kind=kCustom, calls=%fused_computation.2 | custom fusion | bytes 3170304 | tf_op jit(solution)/shard_map/gather | solution.py:99
  113.1 4.1 %broadcast_select_fusion = bf16[128,48,128]{2,1,0:T(8,128)(2,1)} fusion(bf16[128,48,128]{2,1,0:T(8,128)(2,1)} %bitcast.64, pred[128,48]{1,0:T(8,128)(4,1)S(1)} %iota_compare_fusion.4), kind=kLoop, calls=%fused_computation.37 | loop fusion | flops 786432 | bytes 3151872 | tf_op jit(solution)/shard_map/jit(_where)/select_n | solution.py:99
  117.1 10.2 %all-to-all-start.1 = ((bf16[128,48,128]{2,1,0:T(8,128)(2,1)}), bf16[128,48,128]{2,1,0:T(8,128)(2,1)}, u32[]{:S(2)}, u32[]{:S(2)}) async-start(bf16[128,48,128]{2,1,0:T(8,128)(2,1)} %broadcast_select_fusion), calls=%async_computation.1 | async-start | bytes 3145728 | tf_op jit(solution)/shard_map/all_to_all | solution.py:102
  127.4 2.0 fusion.43
  129.6 1.8 fusion.56
  131.4 1.8 copy.46
  133.2 4.3 %collective-permute-start.2 = (f32[2,72,16,1]{1,2,3,0:T(8,128)S(1)}, f32[2,72,16,1]{1,2,3,0:T(8,128)S(1)}, u32[]{:S(2)}, u32[]{:S(2)}) collective-permute-start(f32[2,72,16,1]{1,2,3,0:T(8,128)S(1)} %copy.46), channel_id=1, source_target_pairs={{1,0},{2,1},{3,2},{4,3},{5,4},{6,5},{7,6},{8,7},{9,8},{10,9},{11,1... | collective-permute-start | bytes 27656 | tf_op jit(solution)/shard_map/ppermute | solution.py:33
  137.6 1.7 copy.50
  139.3 0.8 fusion.57
  140.1 3.0 %collective-permute-start.1 = (f32[2,72,1,128]{3,2,1,0:T(1,128)}, f32[2,72,1,128]{3,2,1,0:T(1,128)}, u32[]{:S(2)}, u32[]{:S(2)}) collective-permute-start(f32[2,72,1,128]{3,2,1,0:T(1,128)} %get-tuple-element.127), channel_id=1, source_target_pairs={{16,0},{32,16},{48,32},{64,48},{80,64},{96,80},{112,96},{0,112},{1... | collective-permute-start | bytes 221192 | tf_op jit(solution)/shard_map/ppermute | solution.py:33
  143.1 1.0 slice.106
  144.1 1.3 copy.64
  145.5 2.1 select_maximum_fusion
  147.6 1.6 slice.111
  149.2 3.3 %collective-permute-done.3 = f32[72,16,1]{0,1,2:T(8,128)} collective-permute-done((f32[72,16,1]{0,1,2:T(8,128)S(1)}, f32[72,16,1]{0,1,2:T(8,128)}, u32[]{:S(2)}, u32[]{:S(2)}) %collective-permute-start.3) | collective-permute-done | bytes 4640 | tf_op jit(solution)/shard_map/ppermute | solution.py:15
  152.5 1.5 collective-permute-start.5
  154.0 1.8 copy.49
  155.8 2.2 maximum_minimum_fusion
  158.0 1.5 copy.47
  159.5 1.5 copy.51
  162.4 1.0 maximum_minimum_fusion.1
  163.3 6.5 %reshape.518 = bf16[8,768,2,64]{3,2,1,0:T(2,128)(2,1)} reshape(bf16[128,48,128]{2,1,0:T(8,128)(2,1)} %all-to-all-done.1) | data formatting | bytes 3145728 | tf_op jit(solution)/shard_map/reshape | solution.py:106
  169.8 8.2 %copy.54 = bf16[8,768,2,64]{1,3,2,0:T(8,128)(2,1)} copy(bf16[8,768,2,64]{3,2,1,0:T(2,128)(2,1)} %reshape.518) | data formatting | bytes 3145728
  178.0 41.5 %while.13 = (s32[]{:T(128)}, f32[144,2048]{1,0:T(8,128)}, s32[8,768]{1,0:T(8,128)S(1)}, bf16[8,768,2,64]{1,3,2,0:T(8,128)(2,1)}, s32[]{:T(128)}, /*index=5*/s32[]{:T(128)}) while((s32[]{:T(128)}, f32[144,2048]{1,0:T(8,128)}, s32[8,768]{1,0:T(8,128)S(1)}, bf16[8,768,2,64]{1,3,2,0:T(8,128)(2,1)}, s32[]{:T(128)}, ...), condition=%wide.region_2.3_spmd.clone, body=%wide.region_1.2_spmd.clone.sunk | while | flops 456172800 | bytes 3429975 | solution.py:126
  178.1 0.9 dynamic-slice_bitcast_fusion.2
  179.5 2.6 %fusion.68 = f32[144,2048]{1,0:T(8,128)} fusion(bf16[144,768]{1,0:T(8,128)(2,1)S(1)} %bitcast.65, s32[768]{0:T(1024)S(1)} %fusion.67, f32[144,2048]{1,0:T(8,128)} %get-tuple-element.187, pred[]{:T(512)S(6)} %compare.106), kind=kOutput, calls=%fused_computation.7.clone.1 | convolution fusion | flops 455147520 | bytes 2583553 | tf_op jit(solution)/shard_map/while/body/eval_jaxpr/dot_general | solution.py:121
  182.2 0.9 dynamic-slice_bitcast_fusion.2
  183.5 3.9 %fusion.68 = f32[144,2048]{1,0:T(8,128)} fusion(bf16[144,768]{1,0:T(8,128)(2,1)S(1)} %bitcast.65, s32[768]{0:T(1024)S(1)} %fusion.67, f32[144,2048]{1,0:T(8,128)} %get-tuple-element.187, pred[]{:T(512)S(6)} %compare.106), kind=kOutput, calls=%fused_computation.7.clone.1 | convolution fusion | flops 455147520 | bytes 2583553 | tf_op jit(solution)/shard_map/while/body/eval_jaxpr/dot_general | solution.py:121
  187.5 0.9 dynamic-slice_bitcast_fusion.2
  188.9 3.9 %fusion.68 = f32[144,2048]{1,0:T(8,128)} fusion(bf16[144,768]{1,0:T(8,128)(2,1)S(1)} %bitcast.65, s32[768]{0:T(1024)S(1)} %fusion.67, f32[144,2048]{1,0:T(8,128)} %get-tuple-element.187, pred[]{:T(512)S(6)} %compare.106), kind=kOutput, calls=%fused_computation.7.clone.1 | convolution fusion | flops 455147520 | bytes 2583553 | tf_op jit(solution)/shard_map/while/body/eval_jaxpr/dot_general | solution.py:121
  192.8 0.9 dynamic-slice_bitcast_fusion.2
  194.2 3.9 %fusion.68 = f32[144,2048]{1,0:T(8,128)} fusion(bf16[144,768]{1,0:T(8,128)(2,1)S(1)} %bitcast.65, s32[768]{0:T(1024)S(1)} %fusion.67, f32[144,2048]{1,0:T(8,128)} %get-tuple-element.187, pred[]{:T(512)S(6)} %compare.106), kind=kOutput, calls=%fused_computation.7.clone.1 | convolution fusion | flops 455147520 | bytes 2583553 | tf_op jit(solution)/shard_map/while/body/eval_jaxpr/dot_general | solution.py:121
  198.2 0.9 dynamic-slice_bitcast_fusion.2
  199.6 3.9 %fusion.68 = f32[144,2048]{1,0:T(8,128)} fusion(bf16[144,768]{1,0:T(8,128)(2,1)S(1)} %bitcast.65, s32[768]{0:T(1024)S(1)} %fusion.67, f32[144,2048]{1,0:T(8,128)} %get-tuple-element.187, pred[]{:T(512)S(6)} %compare.106), kind=kOutput, calls=%fused_computation.7.clone.1 | convolution fusion | flops 455147520 | bytes 2583553 | tf_op jit(solution)/shard_map/while/body/eval_jaxpr/dot_general | solution.py:121
  203.5 0.9 dynamic-slice_bitcast_fusion.2
  204.9 3.9 %fusion.68 = f32[144,2048]{1,0:T(8,128)} fusion(bf16[144,768]{1,0:T(8,128)(2,1)S(1)} %bitcast.65, s32[768]{0:T(1024)S(1)} %fusion.67, f32[144,2048]{1,0:T(8,128)} %get-tuple-element.187, pred[]{:T(512)S(6)} %compare.106), kind=kOutput, calls=%fused_computation.7.clone.1 | convolution fusion | flops 455147520 | bytes 2583553 | tf_op jit(solution)/shard_map/while/body/eval_jaxpr/dot_general | solution.py:121
  208.9 0.9 dynamic-slice_bitcast_fusion.2
  210.2 3.9 %fusion.68 = f32[144,2048]{1,0:T(8,128)} fusion(bf16[144,768]{1,0:T(8,128)(2,1)S(1)} %bitcast.65, s32[768]{0:T(1024)S(1)} %fusion.67, f32[144,2048]{1,0:T(8,128)} %get-tuple-element.187, pred[]{:T(512)S(6)} %compare.106), kind=kOutput, calls=%fused_computation.7.clone.1 | convolution fusion | flops 455147520 | bytes 2583553 | tf_op jit(solution)/shard_map/while/body/eval_jaxpr/dot_general | solution.py:121
  214.2 0.9 dynamic-slice_bitcast_fusion.2
  215.6 3.9 %fusion.68 = f32[144,2048]{1,0:T(8,128)} fusion(bf16[144,768]{1,0:T(8,128)(2,1)S(1)} %bitcast.65, s32[768]{0:T(1024)S(1)} %fusion.67, f32[144,2048]{1,0:T(8,128)} %get-tuple-element.187, pred[]{:T(512)S(6)} %compare.106), kind=kOutput, calls=%fused_computation.7.clone.1 | convolution fusion | flops 455147520 | bytes 2583553 | tf_op jit(solution)/shard_map/while/body/eval_jaxpr/dot_general | solution.py:121
  219.5 1.6 copy.66
  221.4 4.0 %bitcast_add_fusion = f32[2,72,16,128]{3,2,1,0:T(8,128)} fusion(f32[2,72,16,128]{3,2,1,0:T(8,128)S(1)} %bitcast.63, f32[2,72,1,128]{3,2,1,0:T(1,128)} %collective-permute-done, f32[2,72,1,128]{3,2,1,0:T(1,128)} %collective-permute-done.1, f32[2,72,16,1]{3,2,1,0:T(8,128)} %copy.51, f32[2,72,16,1]{3,2,1,0:T(8,128)} %copy.47, f32[72,16,128]{2,1,0:T(8,128)S(1)} %copy-done.6, ...), kind=kLoop, calls=%fused_computation.38 | loop fusion | flops 7962624 | bytes 6064128 | tf_op jit(solution)/shard_map/add | solution.py:129
  225.4 2.4 reshape.520
  227.8 2.9 %fusion.10 = f32[2,72,2048]{2,1,0:T(8,128)S(1)} fusion(f32[2,72,2048]{2,1,0:T(8,128)} %reshape.520, f32[2048]{0:T(1024)S(1)} %bitcast.73, f32[72,72]{1,0:T(8,128)S(1)} %copy-done.10), kind=kOutput, calls=%fused_computation.33 | convolution fusion | flops 255393792 | bytes 2388224 | tf_op jit(solution)/shard_map/lk,tlc->tkc/dot_general | solution.py:47
  232.0 0.8 fusion.53
  232.7 1.3 collective-permute-start.6
  234.0 1.7 collective-permute-start.7
  235.7 1.8 fusion.52
  237.5 1.7 copy.56
  239.2 2.1 collective-permute-start.8
  241.3 1.7 copy.58
  243.1 1.5 copy.57
  244.6 5.5 %collective-permute-done.9 = f32[2,72,16,1]{1,2,3,0:T(8,128)S(1)} collective-permute-done((f32[2,72,16,1]{1,2,3,0:T(8,128)S(1)}, f32[2,72,16,1]{1,2,3,0:T(8,128)S(1)}, u32[]{:S(2)}, u32[]{:S(2)}) %collective-permute-start.9) | collective-permute-done | bytes 9248 | tf_op jit(solution)/shard_map/ppermute | solution.py:32
  250.1 1.5 copy.59
  251.6 3.3 %fusion.15 = f32[2,72,16,128]{3,2,1,0:T(8,128)S(1)} fusion(f32[2,72,16,128]{3,2,1,0:T(8,128)S(1)} %bitcast.60, f32[2,72,1,128]{3,2,1,0:T(1,128)S(1)} %collective-permute-done.6, f32[2,72,1,128]{3,2,1,0:T(1,128)S(1)} %collective-permute-done.7, f32[2,72,16,1]{3,2,1,0:T(8,128)} %copy.59, f32[2,72,16,1]{3,2,1,0:T(8,128)} %copy.57, ...), kind=kLoop, calls=%fused_computation.42 | loop fusion | flops 7667712 | bytes 4884480 | tf_op jit(solution)/shard_map/add | solution.py:91
  255.0 1.4 fusion.50
  (104 shorter events, 8.8 us)
Async XLA Ops:
  0.6 90.4 %copy-start = (bf16[6144,128]{1,0:T(8,128)(2,1)S(1)}, bf16[6144,128]{1,0:T(8,128)(2,1)}, u32[]{:S(2)}) copy-start(bf16[6144,128]{1,0:T(8,128)(2,1)} %param.18) | copy-start | bytes 4718596
  0.6 2.7 %copy-start.1 = (s32[6144]{0:T(1024)S(1)}, s32[6144]{0:T(1024)}, u32[]{:S(2)}) copy-start(s32[6144]{0:T(1024)} %param.20) | copy-start | bytes 73732
  3.4 34.3 %copy-start.2 = (s32[6144]{0:T(1024)S(1)}, s32[6144]{0:T(1024)}, u32[]{:S(2)}) copy-start(s32[6144]{0:T(1024)} %param.19) | copy-start | bytes 73732
  37.7 34.4 %copy-start.14 = (s32[1,128]{1,0:T(1,128)S(1)}, s32[1,128]{1,0:T(1,128)}, u32[]{:S(2)}) copy-start(s32[1,128]{1,0:T(1,128)} %param.21) | copy-start | bytes 1540
  72.8 44.4 %all-to-all-start = ((s32[128,1,48]{2,1,0:T(1,128)}), s32[128,1,48]{2,1,0:T(1,128)S(1)}, u32[]{:S(2)}, u32[]{:S(2)}) async-start(s32[128,1,48]{2,1,0:T(1,128)} %bitcast.6), calls=%async_computation | async-start | bytes 131072 | tf_op jit(solution)/shard_map/all_to_all | solution.py:103
  83.9 2.4 copy-start.10
  84.0 2.4 copy-start.11
  117.1 10.2 %copy-start.12 = (f32[16,128]{1,0:T(8,128)S(1)}, f32[16,128]{1,0:T(8,128)}, u32[]{:S(2)}) copy-start(f32[16,128]{1,0:T(8,128)} %param.15) | copy-start | bytes 24580
  117.1 46.2 %all-to-all-start.1 = ((bf16[128,48,128]{2,1,0:T(8,128)(2,1)}), bf16[128,48,128]{2,1,0:T(8,128)(2,1)}, u32[]{:S(2)}, u32[]{:S(2)}) async-start(bf16[128,48,128]{2,1,0:T(8,128)(2,1)} %broadcast_select_fusion), calls=%async_computation.1 | async-start | bytes 3145728 | tf_op jit(solution)/shard_map/all_to_all | solution.py:102
  131.4 11.7 %copy-start.7 = (f32[72,16,128]{2,1,0:T(8,128)S(1)}, f32[72,16,128]{2,1,0:T(8,128)}, u32[]{:S(2)}) copy-start(f32[72,16,128]{2,1,0:T(8,128)} %param.13) | copy-start | bytes 1769476
  133.2 24.8 %collective-permute-start.2 = (f32[2,72,16,1]{1,2,3,0:T(8,128)S(1)}, f32[2,72,16,1]{1,2,3,0:T(8,128)S(1)}, u32[]{:S(2)}, u32[]{:S(2)}) collective-permute-start(f32[2,72,16,1]{1,2,3,0:T(8,128)S(1)} %copy.46), channel_id=1, source_target_pairs={{1,0},{2,1},{3,2},{4,3},{5,4},{6,5},{7,6},{8,7},{9,8},{10,9},{11,1... | collective-permute-start | bytes 27656 | tf_op jit(solution)/shard_map/ppermute | solution.py:33
  139.3 20.2 %collective-permute-start.4 = (f32[2,72,16,1]{1,2,3,0:T(8,128)S(1)}, f32[2,72,16,1]{1,2,3,0:T(8,128)S(1)}, u32[]{:S(2)}, u32[]{:S(2)}) collective-permute-start(f32[2,72,16,1]{1,2,3,0:T(8,128)S(1)} %copy.50), channel_id=1, source_target_pairs={{0,1},{1,2},{2,3},{3,4},{4,5},{5,6},{6,7},{7,8},{8,9},{9,10},{10,1... | collective-permute-start | bytes 27656 | tf_op jit(solution)/shard_map/ppermute | solution.py:32
  140.1 81.0 %collective-permute-start = (f32[2,72,1,128]{3,2,1,0:T(1,128)}, f32[2,72,1,128]{3,2,1,0:T(1,128)}, u32[]{:S(2)}, u32[]{:S(2)}) collective-permute-start(f32[2,72,1,128]{3,2,1,0:T(1,128)} %get-tuple-element.128), channel_id=1, source_target_pairs={{0,16},{16,32},{32,48},{48,64},{64,80},{80,96},{96,112},{112,0},{1... | collective-permute-start | bytes 221192 | tf_op jit(solution)/shard_map/ppermute | solution.py:32
  140.1 81.0 %collective-permute-start.1 = (f32[2,72,1,128]{3,2,1,0:T(1,128)}, f32[2,72,1,128]{3,2,1,0:T(1,128)}, u32[]{:S(2)}, u32[]{:S(2)}) collective-permute-start(f32[2,72,1,128]{3,2,1,0:T(1,128)} %get-tuple-element.127), channel_id=1, source_target_pairs={{16,0},{32,16},{48,32},{64,48},{80,64},{96,80},{112,96},{0,112},{1... | collective-permute-start | bytes 221192 | tf_op jit(solution)/shard_map/ppermute | solution.py:33
  145.4 7.1 %collective-permute-start.3 = (f32[72,16,1]{0,1,2:T(8,128)S(1)}, f32[72,16,1]{0,1,2:T(8,128)}, u32[]{:S(2)}, u32[]{:S(2)}) collective-permute-start(f32[72,16,1]{0,1,2:T(8,128)S(1)} %copy.64), channel_id=1, source_target_pairs={{0,1},{1,2},{2,3},{3,4},{4,5},{5,6},{6,7},{7,8},{8,9},{9,10},{10,1... | collective-permute-start | bytes 13832 | tf_op jit(solution)/shard_map/ppermute | solution.py:15
  152.5 9.8 %collective-permute-start.5 = (f32[72,1,128]{2,1,0:T(1,128)}, f32[72,1,128]{2,1,0:T(1,128)S(1)}, u32[]{:S(2)}, u32[]{:S(2)}) collective-permute-start(f32[72,1,128]{2,1,0:T(1,128)} %slice.111), channel_id=1, source_target_pairs={{0,16},{16,32},{32,48},{48,64},{64,80},{80,96},{96,112},{1,17},{17... | collective-permute-start | bytes 110600 | tf_op jit(solution)/shard_map/ppermute | solution.py:21
  158.0 4.4 %copy-start.8 = (f32[72,16,128]{2,1,0:T(8,128)S(1)}, f32[72,16,128]{2,1,0:T(8,128)}, u32[]{:S(2)}) copy-start(f32[72,16,128]{2,1,0:T(8,128)} %param.14) | copy-start | bytes 1769476
  219.5 1.7 copy-start.3
  219.5 1.7 copy-start.4
  219.5 1.8 copy-start.5
  219.5 1.9 copy-start.6
  230.7 0.7 copy-start.13
  232.7 18.9 %collective-permute-start.6 = (f32[2,72,1,128]{3,2,1,0:T(1,128)}, f32[2,72,1,128]{3,2,1,0:T(1,128)S(1)}, u32[]{:S(2)}, u32[]{:S(2)}) collective-permute-start(f32[2,72,1,128]{3,2,1,0:T(1,128)} %get-tuple-element.120), channel_id=1, source_target_pairs={{0,16},{16,32},{32,48},{48,64},{64,80},{80,96},{96,112},{112,0},{1... | collective-permute-start | bytes 221192 | tf_op jit(solution)/shard_map/ppermute | solution.py:32
  234.0 17.6 %collective-permute-start.7 = (f32[2,72,1,128]{3,2,1,0:T(1,128)}, f32[2,72,1,128]{3,2,1,0:T(1,128)S(1)}, u32[]{:S(2)}, u32[]{:S(2)}) collective-permute-start(f32[2,72,1,128]{3,2,1,0:T(1,128)} %get-tuple-element.119), channel_id=1, source_target_pairs={{16,0},{32,16},{48,32},{64,48},{80,64},{96,80},{112,96},{0,112},{1... | collective-permute-start | bytes 221192 | tf_op jit(solution)/shard_map/ppermute | solution.py:33
  239.2 3.8 %collective-permute-start.8 = (f32[2,72,16,1]{1,2,3,0:T(8,128)S(1)}, f32[2,72,16,1]{1,2,3,0:T(8,128)S(1)}, u32[]{:S(2)}, u32[]{:S(2)}) collective-permute-start(f32[2,72,16,1]{1,2,3,0:T(8,128)S(1)} %copy.56), channel_id=1, source_target_pairs={{1,0},{2,1},{3,2},{4,3},{5,4},{6,5},{7,6},{8,7},{9,8},{10,9},{11,1... | collective-permute-start | bytes 27656 | tf_op jit(solution)/shard_map/ppermute | solution.py:33
  243.0 7.1 %collective-permute-start.9 = (f32[2,72,16,1]{1,2,3,0:T(8,128)S(1)}, f32[2,72,16,1]{1,2,3,0:T(8,128)S(1)}, u32[]{:S(2)}, u32[]{:S(2)}) collective-permute-start(f32[2,72,16,1]{1,2,3,0:T(8,128)S(1)} %copy.58), channel_id=1, source_target_pairs={{0,1},{1,2},{2,3},{3,4},{4,5},{5,6},{6,7},{7,8},{8,9},{9,10},{10,1... | collective-permute-start | bytes 27656 | tf_op jit(solution)/shard_map/ppermute | solution.py:32
  254.9 1.4 copy-start.9
where the time goes:
time: 258 us; the launch traced here: 256 us
  local copies, waits for them, and re-layouts  148 us (57%)
  matrix products  35.7 us (14%)
  starting transfers between devices  35.3 us (14%)
  other arithmetic  27 us (10%)
  waiting for transfers between devices  8.85 us (3%)
    gather x1, local copies, waits for them, and re-layouts, local(): sounding_column[row_ids]  34.3 us
    gather x1, local copies, waits for them, and re-layouts, local(): sounding_level[row_ids] * cells + sounding_column[row_ids]  34.3 us
    dot_general x8, matrix products, place_group(): jnp.dot(placed.reshape(TR * LEV, group_rows), selector, preferred_element...  30 us
    gather x1, local copies, waits for them, and re-layouts, local(): sounding_forcing[row_ids]  22.1 us
    unnamed x35, local copies, waits for them, and re-layouts  12.3 us
    all_to_all x1, starting transfers between devices, local(): lax.all_to_all(codes, ('lat', 'lon'), split_axis=0, concat_axis=0, tiled=...  11.1 us
    ppermute x4, starting transfers between devices, padded_2(): lax.ppermute(first, axis, [(b, a) for a, b in up])  11.1 us
    all_to_all x1, starting transfers between devices, local(): lax.all_to_all(blocks, ('lat', 'lon'), split_axis=0, concat_axis=0, tiled...  10.2 us
  transfers between devices with their start and end apart: 12, of which 2 were waited for; matrix products, arithmetic and copies ran while one was open for 48% of the time, Pallas kernels for 0%

commit v1 on v0

v1 whole, which is shorter than its diff:
```python
import jax
import jax.numpy as jnp
from jax import lax
from jax.experimental import pallas as pl
from jax.experimental.pallas import tpu as pltpu
from jax.sharding import PartitionSpec as P

TR = 2
LEV = 72
SPAN = 64
CAP = 48
CLAT = 16
LANES = 128
CHIPS = 64
STRIDE = 45
BLOCK = 2 * CAP + 16
GROUP = 16
GROUPS = CHIPS // GROUP
ROWS = GROUP * CAP
F32 = jnp.float32
BF16 = jnp.bfloat16
MESH = pl.DeviceIdType.MESH


def place():
    lat = lax.axis_index("lat")
    lon = lax.axis_index("lon")
    return lat, lon, lax.rem(lat, 2), (lat // 2) * 16 + lon


def peer_chip(chip, step):
    return jnp.bitwise_xor(chip, lax.rem(step * STRIDE, CHIPS))


def iota(shape, axis):
    return lax.broadcasted_iota(jnp.int32, shape, axis)


def pack_kernel(counts, forcing, column, level, out, rows_f32, codes, starts):
    lat, lon, core, chip = place()

    def prefix(o, total):
        starts[o] = total
        return total + counts[0, o]

    lax.fori_loop(0, 128, prefix, jnp.int32(0))

    def widen(i, carry):
        at = pl.ds(pl.multiple_of(i * 256, 256), 256)
        rows_f32[at, :] = forcing[at, :].astype(F32)
        return carry

    lax.fori_loop(0, forcing.shape[0] // 256, widen, 0)
    codes[0:48, :] = level[...] * 2048 + column[...]
    codes[48:56, :] = jnp.zeros((8, LANES), jnp.int32)
    lane = iota((8, LANES), 1)
    sub = iota((16, LANES), 0)

    def step(i, carry):
        t = peer_chip(chip, i)
        first_lane = lax.rem(i * CAP, LANES)
        slot = jnp.bitwise_and(lane - first_lane, LANES - 1)
        tile = jnp.zeros((16, LANES), F32)
        for dc in range(2):
            owner = ((t // 16) * 2 + dc) * 16 + lax.rem(t, 16)
            start = starts[owner]
            count = counts[0, owner]
            out[i, dc * CAP : (dc + 1) * CAP, :] = rows_f32[pl.ds(start, CAP), :].astype(BF16)
            row = start // LANES
            off = lax.rem(start, LANES)
            turn = lax.rem(first_lane - off + LANES, LANES)
            near = pltpu.roll(jnp.broadcast_to(codes[pl.ds(row, 1), :], (8, LANES)), turn, 1)
            far = pltpu.roll(jnp.broadcast_to(codes[pl.ds(row + 1, 1), :], (8, LANES)), turn, 1)
            code = jnp.where(slot < LANES - off, near, far)
            valid = slot < count
            shift = jnp.where(valid, jnp.right_shift(code, 11), 0)
            lat_row = jnp.where(valid, jnp.bitwise_and(jnp.right_shift(code, 7), 15), -1)
            lon_col = jnp.bitwise_and(code, 127)
            for k, part in enumerate((shift, lat_row, lon_col)):
                part = part.astype(F32)
                both = jnp.concatenate([part, part], axis=0)
                tile = jnp.where(sub == dc * 3 + k, both, tile)
        out[i, 2 * CAP : BLOCK, :] = tile.astype(BF16)
        return carry

    lax.fori_loop(0, CHIPS, step, 0)


def pack(counts, forcing, column, level):
    vmem = pl.BlockSpec(memory_space=pltpu.VMEM)
    return pl.pallas_call(
        pack_kernel,
        out_shape=jax.ShapeDtypeStruct((CHIPS, BLOCK, LANES), BF16),
        in_specs=[pl.BlockSpec(memory_space=pltpu.SMEM), vmem, vmem, vmem],
        out_specs=vmem,
        scratch_shapes=[
            pltpu.VMEM((forcing.shape[0], LANES), F32),
            pltpu.VMEM((56, LANES), jnp.int32),
            pltpu.SMEM((128,), jnp.int32),
        ],
        compiler_params=pltpu.CompilerParams(vmem_limit_bytes=24 << 20),
        name="pack",
    )(counts, forcing, column.reshape(48, LANES), level.reshape(48, LANES))


def main_kernel(
    adj, ce, cn, dif, flx, conv, send,
    out, flux,
    recv, fwd, fwdc, acc, field, gains, mixer, codes, edges, west_in, east_in, cn_edge, cn_south,
    send_sem, recv_sem, fwd_send, fwd_recv, halo_send, halo_recv, self_sem,
):
    lat, lon, core, chip = place()
    north = lax.rem(lat + 1, 8)
    south = lax.rem(lat + 7, 8)
    east = lax.rem(lon + 1, 16)
    west = lax.rem(lon + 15, 16)
    sibling = lat + 1 - 2 * core
    barrier = pltpu.get_barrier_semaphore()

    def peer(i):
        t = peer_chip(chip, i)
        return ((t // 16) * 2 + core, lax.rem(t, 16))

    def greet(i, carry):
        pl.semaphore_signal(barrier, inc=1, device_id=peer(i), device_id_type=MESH)
        return carry

    lax.fori_loop(1, CHIPS, greet, 0)
    for other in (north, south):
        pl.semaphore_signal(barrier, inc=1, device_id=(other, lon), device_id_type=MESH)
    pl.semaphore_wait(barrier, CHIPS + 1)

    def block_copy(i):
        return pltpu.make_async_remote_copy(
            src_ref=send.at[i], dst_ref=recv.at[i], send_sem=send_sem,
            recv_sem=recv_sem.at[i // GROUP], device_id=peer(i), device_id_type=MESH,
        )

    def post(i, carry):
        block_copy(i).start()
        return carry

    lax.fori_loop(1, CHIPS, post, 0)
    own = pltpu.make_async_copy(send.at[0], recv.at[0], self_sem)
    own.start()

    high = conv[...].astype(BF16).astype(F32)
    mixer[...] = jnp.zeros((256, LANES), F32)
    mixer[0:LEV, 0:LEV] = high
    mixer[LEV : 2 * LEV, 0:LEV] = high
    mixer[2 * LEV : 3 * LEV, 0:LEV] = conv[...] - high
    mix = jnp.transpose(mixer[...])[0:LEV].astype(BF16)
    lev2 = iota((LEV, 2 * LANES), 0)
    lane = iota((LEV, LANES), 1)

    def physics(x, f, d):
        x1 = x.astype(BF16).astype(F32)
        stack = jnp.concatenate([x1, x - x1, x1, jnp.zeros((40, 2 * LANES), F32)], axis=0)
        z = jnp.dot(mix, stack.astype(BF16), preferred_element_type=F32)
        m = x + f * z
        above = jnp.where(lev2 == LEV - 1, m, pltpu.roll(m, LEV - 1, 0))
        below = jnp.where(lev2 == 0, m, pltpu.roll(m, 1, 0))
        return m + d * (above - 2.0 * m + below)

    def column_step(e, load):
        def pair(j, packed):
            r0 = 2 * j
            f = jnp.concatenate([flx[pl.ds(r0, 1), :], flx[pl.ds(r0 + 1, 1), :]], axis=1)
            d = jnp.concatenate([dif[pl.ds(r0, 1), :], dif[pl.ds(r0 + 1, 1), :]], axis=1)
            for t in range(TR):
                x = jnp.concatenate([load(t, r0), load(t, r0 + 1)], axis=1)
                y = physics(x, f, d)
                for k in range(2):
                    part = y[:, k * LANES : (k + 1) * LANES]
                    field[e, r0 + k + 1, t * LEV : (t + 1) * LEV, :] = part
                    at = 2 * (t * CLAT + r0 + k)
                    turned = pltpu.roll(part, at + 1, 1)
                    packed = jnp.where((lane == at) | (lane == at + 1), turned, packed)
            return packed

        return lax.fori_loop(0, CLAT // 2, pair, jnp.zeros((LEV, LANES), F32))

    def halo_copies(e):
        def rc(src, dst, k, dev):
            return pltpu.make_async_remote_copy(
                src_ref=src, dst_ref=dst, send_sem=halo_send.at[e, k],
                recv_sem=halo_recv.at[e, k], device_id=dev, device_id_type=MESH,
            )

        return [
            rc(edges.at[e], west_in.at[e], 0, (lat, east)),
            rc(edges.at[e], east_in.at[e], 1, (lat, west)),
            rc(field.at[e, CLAT], field.at[e, 0], 2, (north, lon)),
            rc(field.at[e, 1], field.at[e, CLAT + 1], 3, (south, lon)),
        ] + ([rc(cn_edge, cn_south, 4, (north, lon))] if e == 0 else [])

    def merged(e):
        return jnp.where(
            jnp.bitwise_and(lane, 1) == 0, west_in[e], pltpu.roll(east_in[e], LANES - 2, 1)
        )

    def advected(e, r, t, halo, g):
        at = 2 * (t * CLAT + r)
        turned = pltpu.roll(halo, lax.rem(2 * LANES - at, LANES), 1)
        rows = pl.ds(t * LEV, LEV)
        c = field[e, r + 1, rows, :]
        n = field[e, r + 2, rows, :]
        s = field[e, r, rows, :]
        ea = jnp.where(lane == LANES - 1, turned, pltpu.roll(c, LANES - 1, 1))
        we = jnp.where(lane == 0, turned, pltpu.roll(c, 1, 1))
        return c + g[0] * (ea - c) + g[1] * (c - we) + g[2] * (n - c) + g[3] * (c - s)

    packed = column_step(0, lambda t, r: adj[pl.ds(t * LEV * CLAT + r, LEV, stride=CLAT), :])

    def face_edge(r, packed):
        at = 64 + 2 * r
        turned = pltpu.roll(ce[pl.ds(r, LEV, stride=CLAT), :], at + 1, 1)
        return jnp.where(lane == at, turned, packed)

    edges[0] = lax.fori_loop(0, CLAT, face_edge, packed)
    cn_edge[...] = cn[pl.ds(CLAT - 1, LEV, stride=CLAT), :]
    first_halo = halo_copies(0)
    for copy in first_halo:
        copy.start()
    for copy in first_halo:
        copy.wait()
    halo0 = merged(0)

    def first_row(r, carry):
        e_face = ce[pl.ds(r, LEV, stride=CLAT), :]
        turned = pltpu.roll(halo0, lax.rem(2 * LANES - 64 - 2 * r, LANES), 1)
        w_face = jnp.where(lane == 0, turned, pltpu.roll(e_face, 1, 1))
        n_face = cn[pl.ds(r, LEV, stride=CLAT), :]
        top = jnp.logical_and(lat == 7, r == CLAT - 1)
        n_face = jnp.where(top, 0.0, n_face)
        s_face = jnp.where(r == 0, cn_south[...], cn[pl.ds(jnp.maximum(r - 1, 0), LEV, stride=CLAT), :])
        s_face = jnp.where(jnp.logical_and(lat == 0, r == 0), 0.0, s_face)
        g = (
            jnp.maximum(e_face, 0.0), jnp.minimum(w_face, 0.0),
            jnp.maximum(n_face, 0.0), jnp.minimum(s_face, 0.0),
        )
        for k in range(4):
            gains[k, r] = g[k]
        for t in range(TR):
            acc[r, t * LEV : (t + 1) * LEV, :] = advected(0, r, t, halo0, g)
        return carry

    lax.fori_loop(0, CLAT, first_row, 0)

    row_id = iota((LANES, LANES), 0)
    eye = (row_id == iota((LANES, LANES), 1)).astype(F32).astype(BF16)
    cell = iota((LANES, ROWS), 0).astype(F32)
    clane = iota((16, LANES), 1)

    def place_group(blocks, tiles):
        parts = []
        for h in range(GROUP // 8):
            s = [tiles[h * 8 + k].astype(F32) for k in range(8)]
            parts.append(jnp.where(clane < 48, s[0], jnp.where(clane < 96, s[1], s[2])))
            parts.append(
                jnp.where(clane < 16, s[2], jnp.where(clane < 64, s[3], jnp.where(clane < 112, s[4], s[5])))
            )
            parts.append(jnp.where(clane < 32, s[5], jnp.where(clane < 80, s[6], s[7])))
        codes[...] = jnp.concatenate(parts, axis=1)
        shift = codes[pl.ds(core * 3, 1), :].astype(jnp.int32)
        lat_row = codes[pl.ds(core * 3 + 1, 1), :]
        lon_col = codes[pl.ds(core * 3 + 2, 1), :]
        turned = lax.dot_general(eye, blocks, (((1,), (1,)), ((), ())), preferred_element_type=F32)
        placed = []
        for t in range(TR):
            x = jnp.concatenate([turned[t * SPAN : (t + 1) * SPAN], jnp.zeros((8, ROWS), F32)], axis=0)
            for bit in (1, 2, 4):
                x = jnp.where(jnp.bitwise_and(shift, bit) != 0, pltpu.roll(x, bit, 0), x)
            x8 = jnp.concatenate([jnp.zeros((8, ROWS), F32), x[: LEV - 8]], axis=0)
            placed.append(jnp.where(jnp.bitwise_and(shift, 8) != 0, x8, x))
        placed = jnp.concatenate(placed, axis=0).astype(BF16)
        hot = jnp.where(cell == lon_col, 1.0, 0.0).astype(BF16)

        def rows_pair(j, carry):
            two = []
            for k in range(2):
                mine = jnp.where(lat_row == (2 * j + k).astype(F32), 1.0, 0.0).astype(BF16)
                two.append(hot * mine)
            res = lax.dot_general(
                placed, jnp.concatenate(two, axis=0), (((1,), (1,)), ((), ())),
                preferred_element_type=F32,
            )
            acc[2 * j] += res[:, :LANES]
            acc[2 * j + 1] += res[:, LANES:]
            return carry

        lax.fori_loop(0, CLAT // 2, rows_pair, 0)

    mine_at = pl.ds(pl.multiple_of(core * CAP, 16), CAP)
    other_at = pl.ds(pl.multiple_of(CAP - core * CAP, 16), CAP)

    def forwards(g):
        at = pl.ds(g * GROUP, GROUP)
        return [
            pltpu.make_async_remote_copy(
                src_ref=recv.at[at, other_at, :], dst_ref=fwd.at[at],
                send_sem=fwd_send.at[0, g], recv_sem=fwd_recv.at[0, g],
                device_id=(sibling, lon), device_id_type=MESH,
            ),
            pltpu.make_async_remote_copy(
                src_ref=recv.at[at, 2 * CAP : BLOCK, :], dst_ref=fwdc.at[at],
                send_sem=fwd_send.at[1, g], recv_sem=fwd_recv.at[1, g],
                device_id=(sibling, lon), device_id_type=MESH,
            ),
        ]

    def arrived(g, lo):
        at = pl.ds(g * GROUP + lo, GROUP - lo)
        pltpu.make_async_remote_copy(
            src_ref=send.at[at], dst_ref=recv.at[at], send_sem=send_sem,
            recv_sem=recv_sem.at[g], device_id=(sibling, lon), device_id_type=MESH,
        ).wait_recv()

    own.wait()
    for g in range(GROUPS):
        arrived(g, 1 if g == 0 else 0)
        for copy in forwards(g):
            copy.start()
        at = pl.ds(g * GROUP, GROUP)
        place_group(recv[at, mine_at, :].reshape(ROWS, LANES), recv[at, 2 * CAP : BLOCK, :])
    for g in range(GROUPS):
        for copy in forwards(g):
            copy.wait_recv()
        at = pl.ds(g * GROUP, GROUP)
        place_group(fwd[at].reshape(ROWS, LANES), fwdc[at])

    edges[1] = column_step(1, lambda t, r: acc[r, t * LEV : (t + 1) * LEV, :])
    second_halo = halo_copies(1)
    for copy in second_halo:
        copy.start()
    for copy in second_halo:
        copy.wait()
    halo1 = merged(1)

    def second_row(r, carry):
        g = tuple(gains[k, r] for k in range(4))
        for t in range(TR):
            y = advected(1, r, t, halo1, g)
            out[pl.ds(t * LEV * CLAT + r, LEV, stride=CLAT), :] = y
            flux[pl.ds(t * CLAT + r, 1), :] = y[0:1] + acc[r, t * LEV : t * LEV + 1, :]
        return carry

    lax.fori_loop(0, CLAT, second_row, 0)
    for g in range(GROUPS):
        for copy in forwards(g):
            copy.wait_send()
    every = pl.ds(1, CHIPS - 1)
    pltpu.make_async_remote_copy(
        src_ref=send.at[every], dst_ref=recv.at[every], send_sem=send_sem,
        recv_sem=recv_sem.at[0], device_id=(sibling, lon), device_id_type=MESH,
    ).wait_send()


def local(adjoint_state, courant_east, courant_north, diffusion, convective_flux, convection,
          sounding_forcing, sounding_column, sounding_level, owner_counts):
    send = pack(owner_counts, sounding_forcing, sounding_column, sounding_level)
    vmem = pl.BlockSpec(memory_space=pltpu.VMEM)
    dma = pltpu.SemaphoreType.DMA
    out, flux = pl.pallas_call(
        main_kernel,
        out_shape=(
            jax.ShapeDtypeStruct((TR * LEV * CLAT, LANES), F32),
            jax.ShapeDtypeStruct((TR * CLAT, LANES), F32),
        ),
        in_specs=[vmem] * 7,
        out_specs=(vmem, vmem),
        scratch_shapes=[
            pltpu.VMEM((CHIPS, BLOCK, LANES), BF16),
            pltpu.VMEM((CHIPS, CAP, LANES), BF16),
            pltpu.VMEM((CHIPS, 16, LANES), BF16),
            pltpu.VMEM((CLAT, TR * LEV, LANES), F32),
            pltpu.VMEM((2, CLAT + 2, TR * LEV, LANES), F32),
            pltpu.VMEM((4, CLAT, LEV, LANES), F32),
            pltpu.VMEM((256, LANES), F32),
            pltpu.VMEM((16, ROWS), F32),
            pltpu.VMEM((2, LEV, LANES), F32),
            pltpu.VMEM((2, LEV, LANES), F32),
            pltpu.VMEM((2, LEV, LANES), F32),
            pltpu.VMEM((LEV, LANES), F32),
            pltpu.VMEM((LEV, LANES), F32),
            dma,
            dma((GROUPS,)),
            dma((2, GROUPS)),
            dma((2, GROUPS)),
            dma((2, 5)),
            dma((2, 5)),
            dma,
        ],
        compiler_params=pltpu.CompilerParams(
            collective_id=0, has_side_effects=True, vmem_limit_bytes=48 << 20
        ),
        name="transport",
    )(
        adjoint_state.reshape(TR * LEV * CLAT, LANES),
        courant_east.reshape(LEV * CLAT, LANES),
        courant_north.reshape(LEV * CLAT, LANES),
        diffusion, convective_flux, convection, send,
    )
    return out.reshape(TR, LEV, CLAT, LANES), flux.reshape(TR, CLAT, LANES)


def solution(mesh):
    return jax.shard_map(
        local,
        mesh=mesh,
        in_specs=(
            P(None, None, "lat", "lon"),
            P(None, "lat", "lon"),
            P(None, "lat", "lon"),
            P("lat", "lon"),
            P("lat", "lon"),
            P(),
            P(("lat", "lon"), None),
            P(("lat", "lon")),
            P(("lat", "lon")),
            P(("lat", "lon"), None),
        ),
        out_specs=(P(None, None, "lat", "lon"), P(None, "lat", "lon")),
        check_vma=False,
    )
```

time: 258 us -> 83.2 us (0.32)
  local copies, waits for them, and re-layouts: 148 us -> 5.17 us
  Pallas kernels: 0 us -> 77.1 us
  matrix products: 35.7 us -> 0 us
  starting transfers between devices: 35.3 us -> 0 us
  other arithmetic: 27 us -> 0 us
  waiting for transfers between devices: 8.85 us -> 0 us
    gather x3 -> x0, local copies, waits for them, and re-layouts: 90.6 us -> none  [the longest x1 34.3 us: local(): sounding_column[row_ids]]
    pallas_call x0 -> x2, Pallas kernels: none -> 77.1 us  [the longest x1 69.1 us: local(): pl.pallas_call(main_kernel, out_shape=(jax.ShapeDtypeStruct((TR * LEV * C...]
    dot_general x10 -> x0, matrix products: 35.7 us -> none  [the longest x8 30 us: place_group(): jnp.dot(placed.reshape(TR * LEV, group_rows), selector, preferred_element...]
    all_to_all x2 -> x0, starting transfers between devices: 21.4 us -> none  [the longest x1 11.1 us: local(): lax.all_to_all(codes, ('lat', 'lon'), split_axis=0, concat_axis=0, tiled=...]
    slice x14 -> x0, local copies, waits for them, and re-layouts: 16.7 us -> none  [the longest x6 8.66 us: padded_2(): first = lax.slice_in_dim(value, 0, width, axis=dim)]
    ppermute x10 -> x0, starting transfers between devices: 13.9 us -> none  [the longest x4 11.1 us: padded_2(): lax.ppermute(first, axis, [(b, a) for a, b in up])]
    reshape x4 -> x0, local copies, waits for them, and re-layouts: 11.4 us -> none  [the longest x1 6.47 us: local(): got_blocks = got_blocks.reshape(lat_size, group_rows, TR, SPAN)]
    add x6 -> x0, other arithmetic: 11 us -> none  [the longest x1 3.98 us: local(): forced = first + forcing.reshape(TR, LEV, lat_rows, lon_cols)]
  transfers between devices with their start and end apart: 12 -> 0, of which waited for: 2 -> 0; matrix products, arithmetic and copies ran while one was open for 48% -> 0% of each run, Pallas kernels for 0% -> 0%
where the time goes in v1:
time: 83.2 us; the launch traced here: 83 us
  Pallas kernels  77.1 us (93%)
  local copies, waits for them, and re-layouts  5.17 us (6%)
    pallas_call x1, Pallas kernels, local(): pl.pallas_call(main_kernel, out_shape=(jax.ShapeDtypeStruct((TR * LEV * C...  69.1 us
    pallas_call x1, Pallas kernels, pack(): pl.pallas_call(pack_kernel, out_shape=jax.ShapeDtypeStruct((CHIPS, BLOCK,...  7.97 us
    unnamed x22, local copies, waits for them, and re-layouts  5.17 us

profile of v1, /device:TPU:0, one launch (start us, length us, event | category | flops | bytes accessed | tf_op | source)
XLA Modules:
  0.0 83.0 jit_solution(16674992375965056736)
XLA Ops:
  0.6 0.0 copy-start
  0.6 1.4 %copy-done = bf16[6144,128]{1,0:T(8,128)(2,1)S(1)} copy-done((bf16[6144,128]{1,0:T(8,128)(2,1)S(1)}, bf16[6144,128]{1,0:T(8,128)(2,1)}, u32[]{:S(2)}) %copy-start) | copy-done | bytes 1572888
  2.0 0.0 copy-start.5
  2.0 0.7 copy-done.5
  2.8 0.0 copy-start.6
  2.8 0.7 copy-done.6
  3.5 0.0 copy-start.9
  3.5 0.7 copy-done.9
  4.2 0.0 copy-start.1
  4.2 0.0 copy-start.2
  4.2 0.0 copy-start.3
  4.2 0.0 copy-start.4
  4.2 0.0 copy-start.7
  4.2 0.0 copy-start.8
  4.2 8.0 %pack.1.send = bf16[64,112,128]{2,1,0:T(8,128)(2,1)S(1)} custom-call(s32[1,128]{1,0:T(1,128)S(1)} %copy-done.9, bf16[6144,128]{1,0:T(8,128)(2,1)S(1)} %copy-done, s32[48,128]{1,0:T(8,128)S(1)} %bitcast.11, s32[48,128]{1,0:T(8,128)S(1)} %bitcast.12), custom_call_target="tpu_custom_call" | custom-call | tf_op jit(solution)/shard_map/pack/pallas_call | solution.py:91
  12.2 0.0 copy-done.1
  12.2 0.0 copy-done.2
  12.2 0.0 copy-done.3
  12.2 0.0 copy-done.4
  12.2 0.0 copy-done.7
  12.2 0.0 copy-done.8
  12.2 69.1 %transport.1 = (f32[2304,128]{1,0:T(8,128)S(1)}, f32[32,128]{1,0:T(8,128)S(1)}) custom-call(f32[2304,128]{1,0:T(8,128)S(1)} %bitcast.7, f32[1152,128]{1,0:T(8,128)S(1)} %bitcast.9, f32[1152,128]{1,0:T(8,128)S(1)} %bitcast.10, f32[16,128]{1,0:T(8,128)S(1)} %copy-done.7, f32[16,128]{1,0:T(8,128)S(1)} %copy-done.8, f32[72,72]{1,0:T(8,128)S(1)} %copy-done.4, ...), custom_call_target="tpu_custom_call" | custom-call | tf_op jit(solution)/shard_map/transport/pallas_call | solution.py:364
  81.3 1.0 %copy.14 = f32[2,72,16,128]{3,2,1,0:T(8,128)} copy(f32[2,72,16,128]{3,2,1,0:T(8,128)S(1)} %bitcast.8) | data formatting | bytes 2359296
  82.4 0.6 copy.15
Async XLA Ops:
  0.6 1.4 %copy-start = (bf16[6144,128]{1,0:T(8,128)(2,1)S(1)}, bf16[6144,128]{1,0:T(8,128)(2,1)}, u32[]{:S(2)}) copy-start(bf16[6144,128]{1,0:T(8,128)(2,1)} %forcing.1) | copy-start | bytes 4718596
  2.0 0.7 copy-start.5
  2.8 0.7 copy-start.6
  3.5 0.7 copy-start.9
  4.2 8.0 %copy-start.1 = (f32[2,72,16,128]{3,2,1,0:T(8,128)S(1)}, f32[2,72,16,128]{3,2,1,0:T(8,128)}, u32[]{:S(2)}) copy-start(f32[2,72,16,128]{3,2,1,0:T(8,128)} %param.10) | copy-start | bytes 3538948
  4.2 8.0 %copy-start.2 = (f32[72,16,128]{2,1,0:T(8,128)S(1)}, f32[72,16,128]{2,1,0:T(8,128)}, u32[]{:S(2)}) copy-start(f32[72,16,128]{2,1,0:T(8,128)} %param.11) | copy-start | bytes 1769476
  4.2 8.0 %copy-start.3 = (f32[72,16,128]{2,1,0:T(8,128)S(1)}, f32[72,16,128]{2,1,0:T(8,128)}, u32[]{:S(2)}) copy-start(f32[72,16,128]{2,1,0:T(8,128)} %param.12) | copy-start | bytes 1769476
  4.2 8.0 %copy-start.4 = (f32[72,72]{1,0:T(8,128)S(1)}, f32[72,72]{1,0:T(8,128)}, u32[]{:S(2)}) copy-start(f32[72,72]{1,0:T(8,128)} %conv.1) | copy-start | bytes 62212
  4.2 8.0 %copy-start.7 = (f32[16,128]{1,0:T(8,128)S(1)}, f32[16,128]{1,0:T(8,128)}, u32[]{:S(2)}) copy-start(f32[16,128]{1,0:T(8,128)} %dif.1) | copy-start | bytes 24580
  4.2 8.0 %copy-start.8 = (f32[16,128]{1,0:T(8,128)S(1)}, f32[16,128]{1,0:T(8,128)}, u32[]{:S(2)}) copy-start(f32[16,128]{1,0:T(8,128)} %flx.1) | copy-start | bytes 24580

commit v2 on v1

--- a/solution.py
+++ b/solution.py
@@ -36,14 +36,50 @@
     return lax.broadcasted_iota(jnp.int32, shape, axis)
 
 
-def pack_kernel(counts, forcing, column, level, out, rows_f32, codes, starts):
+def main_kernel(
+    counts, adj_hbm, ce_hbm, cn_hbm, dif_hbm, flx_hbm, conv_hbm, forcing_hbm, column_hbm, level_hbm,
+    out, flux,
+    adj, ce, cn, dif, flx, conv, forcing, column, level,
+    rows_f32, targets, starts, load_sem,
+    send, recv, fwd, fwdc, acc, field, gains, mixer, codes, edges, west_in, east_in, cn_edge, cn_south,
+    send_sem, recv_sem, fwd_send, fwd_recv, halo_send, halo_recv, self_sem,
+):
     lat, lon, core, chip = place()
+    north = lax.rem(lat + 1, 8)
+    south = lax.rem(lat + 7, 8)
+    east = lax.rem(lon + 1, 16)
+    west = lax.rem(lon + 15, 16)
+    sibling = lat + 1 - 2 * core
+    loads = [
+        pltpu.make_async_copy(src, dst, load_sem.at[k])
+        for k, (src, dst) in enumerate((
+            (forcing_hbm, forcing), (column_hbm, column), (level_hbm, level), (adj_hbm, adj), (conv_hbm, conv),
+            (dif_hbm, dif), (flx_hbm, flx), (ce_hbm, ce), (cn_hbm, cn),
+        ))
+    ]
+    for copy in loads:
+        copy.start()
+    barrier = pltpu.get_barrier_semaphore()
+
+    def peer(i):
+        t = peer_chip(chip, i)
+        return ((t // 16) * 2 + core, lax.rem(t, 16))
+
+    def greet(i, carry):
+        pl.semaphore_signal(barrier, inc=1, device_id=peer(i), device_id_type=MESH)
+        return carry
+
+    lax.fori_loop(1, CHIPS, greet, 0)
+    for other in (north, south):
+        pl.semaphore_signal(barrier, inc=1, device_id=(other, lon), device_id_type=MESH)
 
     def prefix(o, total):
         starts[o] = total
         return total + counts[0, o]
 
     lax.fori_loop(0, 128, prefix, jnp.int32(0))
+    for copy in loads[:3]:
+        copy.wait()
 
     def widen(i, carry):
         at = pl.ds(pl.multiple_of(i * 256, 256), 256)
@@ -51,26 +87,26 @@
         return carry
 
     lax.fori_loop(0, forcing.shape[0] // 256, widen, 0)
-    codes[0:48, :] = level[...] * 2048 + column[...]
-    codes[48:56, :] = jnp.zeros((8, LANES), jnp.int32)
-    lane = iota((8, LANES), 1)
-    sub = iota((16, LANES), 0)
-
-    def step(i, carry):
+    targets[0:48, :] = level[...] * 2048 + column[...]
+    targets[48:56, :] = jnp.zeros((8, LANES), jnp.int32)
+    lane8 = iota((8, LANES), 1)
+    sub16 = iota((16, LANES), 0)
+
+    def pack(i):
         t = peer_chip(chip, i)
         first_lane = lax.rem(i * CAP, LANES)
-        slot = jnp.bitwise_and(lane - first_lane, LANES - 1)
+        slot = jnp.bitwise_and(lane8 - first_lane, LANES - 1)
         tile = jnp.zeros((16, LANES), F32)
         for dc in range(2):
             owner = ((t // 16) * 2 + dc) * 16 + lax.rem(t, 16)
             start = starts[owner]
             count = counts[0, owner]
-            out[i, dc * CAP : (dc + 1) * CAP, :] = rows_f32[pl.ds(start, CAP), :].astype(BF16)
+            send[i, dc * CAP : (dc + 1) * CAP, :] = rows_f32[pl.ds(start, CAP), :].astype(BF16)
             row = start // LANES
             off = lax.rem(start, LANES)
             turn = lax.rem(first_lane - off + LANES, LANES)
-            near = pltpu.roll(jnp.broadcast_to(codes[pl.ds(row, 1), :], (8, LANES)), turn, 1)
-            far = pltpu.roll(jnp.broadcast_to(codes[pl.ds(row + 1, 1), :], (8, LANES)), turn, 1)
+            near = pltpu.roll(jnp.broadcast_to(targets[pl.ds(row, 1), :], (8, LANES)), turn, 1)
+            far = pltpu.roll(jnp.broadcast_to(targets[pl.ds(row + 1, 1), :], (8, LANES)), turn, 1)
             code = jnp.where(slot < LANES - off, near, far)
             valid = slot < count
             shift = jnp.where(valid, jnp.right_shift(code, 11), 0)
@@ -79,56 +115,8 @@
             for k, part in enumerate((shift, lat_row, lon_col)):
                 part = part.astype(F32)
                 both = jnp.concatenate([part, part], axis=0)
-                tile = jnp.where(sub == dc * 3 + k, both, tile)
-        out[i, 2 * CAP : BLOCK, :] = tile.astype(BF16)
-        return carry
-
-    lax.fori_loop(0, CHIPS, step, 0)
-
-
-def pack(counts, forcing, column, level):
-    vmem = pl.BlockSpec(memory_space=pltpu.VMEM)
-    return pl.pallas_call(
-        pack_kernel,
-        out_shape=jax.ShapeDtypeStruct((CHIPS, BLOCK, LANES), BF16),
-        in_specs=[pl.BlockSpec(memory_space=pltpu.SMEM), vmem, vmem, vmem],
-        out_specs=vmem,
-        scratch_shapes=[
-            pltpu.VMEM((forcing.shape[0], LANES), F32),
-            pltpu.VMEM((56, LANES), jnp.int32),
-            pltpu.SMEM((128,), jnp.int32),
-        ],
-        compiler_params=pltpu.CompilerParams(vmem_limit_bytes=24 << 20),
-        name="pack",
-    )(counts, forcing, column.reshape(48, LANES), level.reshape(48, LANES))
-
-
-def main_kernel(
-    adj, ce, cn, dif, flx, conv, send,
-    out, flux,
-    recv, fwd, fwdc, acc, field, gains, mixer, codes, edges, west_in, east_in, cn_edge, cn_south,
-    send_sem, recv_sem, fwd_send, fwd_recv, halo_send, halo_recv, self_sem,
-):
-    lat, lon, core, chip = place()
-    north = lax.rem(lat + 1, 8)
-    south = lax.rem(lat + 7, 8)
-    east = lax.rem(lon + 1, 16)
-    west = lax.rem(lon + 15, 16)
-    sibling = lat + 1 - 2 * core
-    barrier = pltpu.get_barrier_semaphore()
-
-    def peer(i):
-        t = peer_chip(chip, i)
-        return ((t // 16) * 2 + core, lax.rem(t, 16))
-
-    def greet(i, carry):
-        pl.semaphore_signal(barrier, inc=1, device_id=peer(i), device_id_type=MESH)
-        return carry
-
-    lax.fori_loop(1, CHIPS, greet, 0)
-    for other in (north, south):
-        pl.semaphore_signal(barrier, inc=1, device_id=(other, lon), device_id_type=MESH)
-    pl.semaphore_wait(barrier, CHIPS + 1)
+                tile = jnp.where(sub16 == dc * 3 + k, both, tile)
+        send[i, 2 * CAP : BLOCK, :] = tile.astype(BF16)
 
     def block_copy(i):
         return pltpu.make_async_remote_copy(
@@ -136,13 +124,19 @@
             recv_sem=recv_sem.at[i // GROUP], device_id=peer(i), device_id_type=MESH,
         )
 
+    pack(0)
+    own = pltpu.make_async_copy(send.at[0], recv.at[0], self_sem)
+    own.start()
+    pl.semaphore_wait(barrier, CHIPS + 1)
+
     def post(i, carry):
+        pack(i)
         block_copy(i).start()
         return carry
 
     lax.fori_loop(1, CHIPS, post, 0)
-    own = pltpu.make_async_copy(send.at[0], recv.at[0], self_sem)
-    own.start()
+    for copy in loads[3:]:
+        copy.wait()
 
     high = conv[...].astype(BF16).astype(F32)
     mixer[...] = jnp.zeros((256, LANES), F32)
@@ -249,7 +243,7 @@
 
     row_id = iota((LANES, LANES), 0)
     eye = (row_id == iota((LANES, LANES), 1)).astype(F32).astype(BF16)
-    cell = iota((LANES, ROWS), 0).astype(F32)
+    cells = iota((ROWS, 2 * LANES), 1).astype(F32)
     clane = iota((16, LANES), 1)
 
     def place_group(blocks, tiles):
@@ -274,22 +268,14 @@
             x8 = jnp.concatenate([jnp.zeros((8, ROWS), F32), x[: LEV - 8]], axis=0)
             placed.append(jnp.where(jnp.bitwise_and(shift, 8) != 0, x8, x))
         placed = jnp.concatenate(placed, axis=0).astype(BF16)
-        hot = jnp.where(cell == lon_col, 1.0, 0.0).astype(BF16)
-
-        def rows_pair(j, carry):
-            two = []
-            for k in range(2):
-                mine = jnp.where(lat_row == (2 * j + k).astype(F32), 1.0, 0.0).astype(BF16)
-                two.append(hot * mine)
-            res = lax.dot_general(
-                placed, jnp.concatenate(two, axis=0), (((1,), (1,)), ((), ())),
-                preferred_element_type=F32,
-            )
+        parity = jnp.bitwise_and(lat_row.astype(jnp.int32), 1).astype(F32)
+        cell = jnp.broadcast_to(parity * LANES + lon_col, (8, ROWS))
+        hot = jnp.where(jnp.transpose(cell)[:, 0:1] == cells, 1.0, 0.0).astype(BF16)
+        for j in range(CLAT // 2):
+            mine = jnp.where((lat_row == 2 * j) | (lat_row == 2 * j + 1), 1.0, 0.0).astype(BF16)
+            res = jnp.dot(placed * mine, hot, preferred_element_type=F32)
             acc[2 * j] += res[:, :LANES]
             acc[2 * j + 1] += res[:, LANES:]
-            return carry
-
-        lax.fori_loop(0, CLAT // 2, rows_pair, 0)
 
     mine_at = pl.ds(pl.multiple_of(core * CAP, 16), CAP)
     other_at = pl.ds(pl.multiple_of(CAP - core * CAP, 16), CAP)
@@ -358,18 +344,32 @@
 
 def local(adjoint_state, courant_east, courant_north, diffusion, convective_flux, convection,
           sounding_forcing, sounding_column, sounding_level, owner_counts):
-    send = pack(owner_counts, sounding_forcing, sounding_column, sounding_level)
     vmem = pl.BlockSpec(memory_space=pltpu.VMEM)
     dma = pltpu.SemaphoreType.DMA
+    listed = sounding_forcing.shape[0]
     out, flux = pl.pallas_call(
         main_kernel,
         out_shape=(
             jax.ShapeDtypeStruct((TR * LEV * CLAT, LANES), F32),
             jax.ShapeDtypeStruct((TR * CLAT, LANES), F32),
         ),
-        in_specs=[vmem] * 7,
+        in_specs=[pl.BlockSpec(memory_space=pltpu.SMEM)] + [pl.BlockSpec(memory_space=pl.ANY)] * 9,
         out_specs=(vmem, vmem),
         scratch_shapes=[
+            pltpu.VMEM((TR * LEV * CLAT, LANES), F32),
+            pltpu.VMEM((LEV * CLAT, LANES), F32),
+            pltpu.VMEM((LEV * CLAT, LANES), F32),
+            pltpu.VMEM((CLAT, LANES), F32),
+            pltpu.VMEM((CLAT, LANES), F32),
+            pltpu.VMEM((LEV, LEV), F32),
+            pltpu.VMEM((listed, LANES), BF16),
+            pltpu.VMEM((listed // LANES, LANES), jnp.int32),
+            pltpu.VMEM((listed // LANES, LANES), jnp.int32),
+            pltpu.VMEM((listed, LANES), F32),
+            pltpu.VMEM((56, LANES), jnp.int32),
+            pltpu.SMEM((128,), jnp.int32),
+            dma((9,)),
+            pltpu.VMEM((CHIPS, BLOCK, LANES), BF16),
             pltpu.VMEM((CHIPS, BLOCK, LANES), BF16),
             pltpu.VMEM((CHIPS, CAP, LANES), BF16),
             pltpu.VMEM((CHIPS, 16, LANES), BF16),
@@ -392,14 +392,18 @@
             dma,
         ],
         compiler_params=pltpu.CompilerParams(
-            collective_id=0, has_side_effects=True, vmem_limit_bytes=48 << 20
+            collective_id=0, has_side_effects=True, vmem_limit_bytes=60 << 20
         ),
         name="transport",
     )(
+        owner_counts,
         adjoint_state.reshape(TR * LEV * CLAT, LANES),
         courant_east.reshape(LEV * CLAT, LANES),
         courant_north.reshape(LEV * CLAT, LANES),
-        diffusion, convective_flux, convection, send,
+        diffusion, convective_flux, convection,
+        sounding_forcing,
+        sounding_column.reshape(listed // LANES, LANES),
+        sounding_level.reshape(listed // LANES, LANES),
     )
     return out.reshape(TR, LEV, CLAT, LANES), flux.reshape(TR, CLAT, LANES)
 

time: 83.2 us -> 60 us (0.72)
  Pallas kernels: 77.1 us -> 56.2 us
  local copies, waits for them, and re-layouts: 5.17 us -> 2.97 us
    pallas_call x1, Pallas kernels: 69.1 us -> 56.2 us  [local(): pl.pallas_call(main_kernel, out_shape=(jax.ShapeDtypeStruct((TR * LEV * C...]
    pallas_call x1 -> x0, Pallas kernels: 7.97 us -> none  [pack(): pl.pallas_call(pack_kernel, out_shape=jax.ShapeDtypeStruct((CHIPS, BLOCK,...]
    unnamed x22 -> x4, local copies, waits for them, and re-layouts: 5.17 us -> 2.97 us
where the time goes in v2:
time: 60 us; the launch traced here: 59.8 us
  Pallas kernels  56.2 us (94%)
  local copies, waits for them, and re-layouts  2.97 us (5%)
  between operations  0.65 us (1%)
    pallas_call x1, Pallas kernels, local(): pl.pallas_call(main_kernel, out_shape=(jax.ShapeDtypeStruct((TR * LEV * C...  56.2 us
    unnamed x4, local copies, waits for them, and re-layouts  2.97 us

profile of v2, /device:TPU:0, one launch (start us, length us, event | category | flops | bytes accessed | tf_op | source)
XLA Modules:
  0.0 59.8 jit_solution(9151755374340267026)
XLA Ops:
  0.6 56.2 %transport.1 = (f32[2304,128]{1,0:T(8,128)}, f32[32,128]{1,0:T(8,128)}) custom-call(s32[1,128]{1,0:T(1,128)} %counts.1, f32[2304,128]{1,0:T(8,128)} %bitcast.7, f32[1152,128]{1,0:T(8,128)} %bitcast.9, f32[1152,128]{1,0:T(8,128)} %bitcast.10, f32[16,128]{1,0:T(8,128)} %dif_hbm.1, f32[16,128]{1,0:T(8,128)} %flx_hbm.1, f32[72,72]{1,0:T(8,128)} %conv_hbm.1, ...), custom_call_target="tpu_custom_call" | custom-call | tf_op jit(solution)/shard_map/transport/pallas_call | solution.py:350
  56.8 0.0 copy-start
  56.8 2.4 %copy.14 = f32[2,72,16,128]{3,2,1,0:T(8,128)} copy(f32[2,72,16,128]{3,2,1,0:T(8,128)} %bitcast.8) | data formatting | bytes 2359296
  59.2 0.0 copy-done
  59.2 0.6 %copy.15 = f32[2,16,128]{2,1,0:T(8,128)} copy(f32[2,16,128]{2,1,0:T(8,128)S(1)} %bitcast.13) | data formatting | bytes 32768
Async XLA Ops:
  56.8 2.4 %copy-start = (f32[32,128]{1,0:T(8,128)S(1)}, f32[32,128]{1,0:T(8,128)}, u32[]{:S(2)}) copy-start(f32[32,128]{1,0:T(8,128)} %get-tuple-element.5) | copy-start | bytes 49156

commit v3 on v2

--- a/solution.py
+++ b/solution.py
@@ -25,11 +25,11 @@
 def place():
     lat = lax.axis_index("lat")
     lon = lax.axis_index("lon")
-    return lat, lon, lax.rem(lat, 2), (lat // 2) * 16 + lon
+    return lat, lon, jnp.bitwise_and(lat, 1), jnp.right_shift(lat, 1) * 16 + lon
 
 
 def peer_chip(chip, step):
-    return jnp.bitwise_xor(chip, lax.rem(step * STRIDE, CHIPS))
+    return jnp.bitwise_xor(chip, jnp.bitwise_and(step * STRIDE, CHIPS - 1))
 
 
 def iota(shape, axis):
@@ -63,13 +63,13 @@
 
     def peer(i):
         t = peer_chip(chip, i)
-        return ((t // 16) * 2 + core, lax.rem(t, 16))
+        return (jnp.right_shift(t, 4) * 2 + core, jnp.bitwise_and(t, 15))
 
     def greet(i, carry):
         pl.semaphore_signal(barrier, inc=1, device_id=peer(i), device_id_type=MESH)
         return carry
 
-    lax.fori_loop(1, CHIPS, greet, 0)
+    lax.fori_loop(1, CHIPS, greet, 0, unroll=1)
     for other in (north, south):
         pl.semaphore_signal(barrier, inc=1, device_id=(other, lon), device_id_type=MESH)
 
@@ -77,7 +77,7 @@
         starts[o] = total
         return total + counts[0, o]
 
-    lax.fori_loop(0, 128, prefix, jnp.int32(0))
+    lax.fori_loop(0, 128, prefix, jnp.int32(0), unroll=8)
     for copy in loads[:3]:
         copy.wait()
 
@@ -86,7 +86,7 @@
         rows_f32[at, :] = forcing[at, :].astype(F32)
         return carry
 
-    lax.fori_loop(0, forcing.shape[0] // 256, widen, 0)
+    lax.fori_loop(0, forcing.shape[0] // 256, widen, 0, unroll=2)
     targets[0:48, :] = level[...] * 2048 + column[...]
     targets[48:56, :] = jnp.zeros((8, LANES), jnp.int32)
     lane8 = iota((8, LANES), 1)
@@ -94,17 +94,17 @@
 
     def pack(i):
         t = peer_chip(chip, i)
-        first_lane = lax.rem(i * CAP, LANES)
+        first_lane = jnp.bitwise_and(i * CAP, LANES - 1)
         slot = jnp.bitwise_and(lane8 - first_lane, LANES - 1)
         tile = jnp.zeros((16, LANES), F32)
         for dc in range(2):
-            owner = ((t // 16) * 2 + dc) * 16 + lax.rem(t, 16)
+            owner = (jnp.right_shift(t, 4) * 2 + dc) * 16 + jnp.bitwise_and(t, 15)
             start = starts[owner]
             count = counts[0, owner]
             send[i, dc * CAP : (dc + 1) * CAP, :] = rows_f32[pl.ds(start, CAP), :].astype(BF16)
-            row = start // LANES
-            off = lax.rem(start, LANES)
-            turn = lax.rem(first_lane - off + LANES, LANES)
+            row = jnp.right_shift(start, 7)
+            off = jnp.bitwise_and(start, LANES - 1)
+            turn = jnp.bitwise_and(first_lane - off + LANES, LANES - 1)
             near = pltpu.roll(jnp.broadcast_to(targets[pl.ds(row, 1), :], (8, LANES)), turn, 1)
             far = pltpu.roll(jnp.broadcast_to(targets[pl.ds(row + 1, 1), :], (8, LANES)), turn, 1)
             code = jnp.where(slot < LANES - off, near, far)
@@ -121,7 +121,7 @@
     def block_copy(i):
         return pltpu.make_async_remote_copy(
             src_ref=send.at[i], dst_ref=recv.at[i], send_sem=send_sem,
-            recv_sem=recv_sem.at[i // GROUP], device_id=peer(i), device_id_type=MESH,
+            recv_sem=recv_sem.at[jnp.right_shift(i, 4)], device_id=peer(i), device_id_type=MESH,
         )
 
     pack(0)
@@ -134,7 +134,7 @@
         block_copy(i).start()
         return carry
 
-    lax.fori_loop(1, CHIPS, post, 0)
+    lax.fori_loop(1, CHIPS, post, 0, unroll=1)
     for copy in loads[3:]:
         copy.wait()
 
@@ -172,7 +172,7 @@
                     packed = jnp.where((lane == at) | (lane == at + 1), turned, packed)
             return packed
 
-        return lax.fori_loop(0, CLAT // 2, pair, jnp.zeros((LEV, LANES), F32))
+        return lax.fori_loop(0, CLAT // 2, pair, jnp.zeros((LEV, LANES), F32), unroll=8)
 
     def halo_copies(e):
         def rc(src, dst, k, dev):
@@ -211,16 +211,13 @@
         turned = pltpu.roll(ce[pl.ds(r, LEV, stride=CLAT), :], at + 1, 1)
         return jnp.where(lane == at, turned, packed)
 
-    edges[0] = lax.fori_loop(0, CLAT, face_edge, packed)
+    edges[0] = lax.fori_loop(0, CLAT, face_edge, packed, unroll=True)
     cn_edge[...] = cn[pl.ds(CLAT - 1, LEV, stride=CLAT), :]
     first_halo = halo_copies(0)
     for copy in first_halo:
         copy.start()
-    for copy in first_halo:
-        copy.wait()
-    halo0 = merged(0)
-
-    def first_row(r, carry):
+
+    def first_row(r, halo0):
         e_face = ce[pl.ds(r, LEV, stride=CLAT), :]
         turned = pltpu.roll(halo0, lax.rem(2 * LANES - 64 - 2 * r, LANES), 1)
         w_face = jnp.where(lane == 0, turned, pltpu.roll(e_face, 1, 1))
@@ -236,17 +233,15 @@
         for k in range(4):
             gains[k, r] = g[k]
         for t in range(TR):
-            acc[r, t * LEV : (t + 1) * LEV, :] = advected(0, r, t, halo0, g)
-        return carry
-
-    lax.fori_loop(0, CLAT, first_row, 0)
+            acc[r, t * LEV : (t + 1) * LEV, :] += advected(0, r, t, halo0, g)
+        return halo0
 
     row_id = iota((LANES, LANES), 0)
     eye = (row_id == iota((LANES, LANES), 1)).astype(F32).astype(BF16)
     cells = iota((ROWS, 2 * LANES), 1).astype(F32)
     clane = iota((16, LANES), 1)
 
-    def place_group(blocks, tiles):
+    def place_group(blocks, tiles, fresh=False):
         parts = []
         for h in range(GROUP // 8):
             s = [tiles[h * 8 + k].astype(F32) for k in range(8)]
@@ -274,8 +269,12 @@
         for j in range(CLAT // 2):
             mine = jnp.where((lat_row == 2 * j) | (lat_row == 2 * j + 1), 1.0, 0.0).astype(BF16)
             res = jnp.dot(placed * mine, hot, preferred_element_type=F32)
-            acc[2 * j] += res[:, :LANES]
-            acc[2 * j + 1] += res[:, LANES:]
+            if fresh:
+                acc[2 * j] = res[:, :LANES]
+                acc[2 * j + 1] = res[:, LANES:]
+            else:
+                acc[2 * j] += res[:, :LANES]
+                acc[2 * j + 1] += res[:, LANES:]
 
     mine_at = pl.ds(pl.multiple_of(core * CAP, 16), CAP)
     other_at = pl.ds(pl.multiple_of(CAP - core * CAP, 16), CAP)
@@ -302,18 +301,38 @@
             recv_sem=recv_sem.at[g], device_id=(sibling, lon), device_id_type=MESH,
         ).wait_recv()
 
-    own.wait()
-    for g in range(GROUPS):
-        arrived(g, 1 if g == 0 else 0)
-        for copy in forwards(g):
-            copy.start()
+    def place_direct(g):
         at = pl.ds(g * GROUP, GROUP)
-        place_group(recv[at, mine_at, :].reshape(ROWS, LANES), recv[at, 2 * CAP : BLOCK, :])
-    for g in range(GROUPS):
+        place_group(recv[at, mine_at, :].reshape(ROWS, LANES), recv[at, 2 * CAP : BLOCK, :], g == 0)
+
+    def place_forwarded(g):
         for copy in forwards(g):
             copy.wait_recv()
         at = pl.ds(g * GROUP, GROUP)
         place_group(fwd[at].reshape(ROWS, LANES), fwdc[at])
+
+    own.wait()
+
+    def take(g):
+        arrived(g, 1 if g == 0 else 0)
+        for copy in forwards(g):
+            copy.start()
+        place_direct(g)
+
+    def finish_first():
+        for copy in first_halo:
+            copy.wait()
+        lax.fori_loop(0, CLAT, first_row, merged(0), unroll=4)
+
+    take(0)
+    take(1)
+    place_forwarded(0)
+    take(2)
+    place_forwarded(1)
+    place_forwarded(2)
+    take(3)
+    finish_first()
+    place_forwarded(3)
 
     edges[1] = column_step(1, lambda t, r: acc[r, t * LEV : (t + 1) * LEV, :])
     second_halo = halo_copies(1)
@@ -331,7 +350,7 @@
             flux[pl.ds(t * CLAT + r, 1), :] = y[0:1] + acc[r, t * LEV : t * LEV + 1, :]
         return carry
 
-    lax.fori_loop(0, CLAT, second_row, 0)
+    lax.fori_loop(0, CLAT, second_row, 0, unroll=4)
     for g in range(GROUPS):
         for copy in forwards(g):
             copy.wait_send()

time: 60 us -> 50.3 us (0.84)
  Pallas kernels: 56.2 us -> 46.5 us
    pallas_call x1, Pallas kernels: 56.2 us -> 46.5 us  [local(): pl.pallas_call(main_kernel, out_shape=(jax.ShapeDtypeStruct((TR * LEV * C...]
where the time goes in v3:
time: 50.3 us; the launch traced here: 50.1 us
  Pallas kernels  46.5 us (92%)
  local copies, waits for them, and re-layouts  2.97 us (6%)
  between operations  0.65 us (1%)
    pallas_call x1, Pallas kernels, local(): pl.pallas_call(main_kernel, out_shape=(jax.ShapeDtypeStruct((TR * LEV * C...  46.5 us
    unnamed x4, local copies, waits for them, and re-layouts  2.97 us

profile of v3, /device:TPU:0, one launch (start us, length us, event | category | flops | bytes accessed | tf_op | source)
XLA Modules:
  0.0 50.1 jit_solution(5553456572223976430)
XLA Ops:
  0.6 46.5 %transport.1 = (f32[2304,128]{1,0:T(8,128)}, f32[32,128]{1,0:T(8,128)}) custom-call(s32[1,128]{1,0:T(1,128)} %counts.1, f32[2304,128]{1,0:T(8,128)} %bitcast.7, f32[1152,128]{1,0:T(8,128)} %bitcast.9, f32[1152,128]{1,0:T(8,128)} %bitcast.10, f32[16,128]{1,0:T(8,128)} %dif_hbm.1, f32[16,128]{1,0:T(8,128)} %flx_hbm.1, f32[72,72]{1,0:T(8,128)} %conv_hbm.1, ...), custom_call_target="tpu_custom_call" | custom-call | tf_op jit(solution)/shard_map/transport/pallas_call | solution.py:369
  47.1 0.0 copy-start
  47.1 2.4 %copy.14 = f32[2,72,16,128]{3,2,1,0:T(8,128)} copy(f32[2,72,16,128]{3,2,1,0:T(8,128)} %bitcast.8) | data formatting | bytes 2359296
  49.5 0.0 copy-done
  49.5 0.6 %copy.15 = f32[2,16,128]{2,1,0:T(8,128)} copy(f32[2,16,128]{2,1,0:T(8,128)S(1)} %bitcast.13) | data formatting | bytes 32768
Async XLA Ops:
  47.1 2.4 %copy-start = (f32[32,128]{1,0:T(8,128)S(1)}, f32[32,128]{1,0:T(8,128)}, u32[]{:S(2)}) copy-start(f32[32,128]{1,0:T(8,128)} %get-tuple-element.5) | copy-start | bytes 49156

commit v4 on v3

--- a/solution.py
+++ b/solution.py
@@ -13,12 +13,12 @@
 LANES = 128
 CHIPS = 64
 STRIDE = 45
-BLOCK = 2 * CAP + 16
-GROUP = 16
-GROUPS = CHIPS // GROUP
-ROWS = GROUP * CAP
+TILES = CAP // 8
+BLOCK = 2 * TILES + 1
+GROUPS = ((0, 16), (16, 16), (32, 16), (48, 8), (56, 8))
 F32 = jnp.float32
 BF16 = jnp.bfloat16
+COPIES = 4
 MESH = pl.DeviceIdType.MESH
 
 
@@ -57,7 +57,7 @@
             (dif_hbm, dif), (flx_hbm, flx), (ce_hbm, ce), (cn_hbm, cn),
         ))
     ]
-    for copy in loads:
+    for copy in loads[:3]:
         copy.start()
     barrier = pltpu.get_barrier_semaphore()
 
@@ -69,9 +69,12 @@
         pl.semaphore_signal(barrier, inc=1, device_id=peer(i), device_id_type=MESH)
         return carry
 
-    lax.fori_loop(1, CHIPS, greet, 0, unroll=1)
+    lax.fori_loop(1, CHIPS, greet, 0, unroll=7)
     for other in (north, south):
         pl.semaphore_signal(barrier, inc=1, device_id=(other, lon), device_id_type=MESH)
+
+    for copy in loads[3:]:
+        copy.start()
 
     def prefix(o, total):
         starts[o] = total
@@ -90,18 +93,19 @@
     targets[0:48, :] = level[...] * 2048 + column[...]
     targets[48:56, :] = jnp.zeros((8, LANES), jnp.int32)
     lane8 = iota((8, LANES), 1)
-    sub16 = iota((16, LANES), 0)
+    sub8 = iota((8, LANES), 0)
 
     def pack(i):
         t = peer_chip(chip, i)
         first_lane = jnp.bitwise_and(i * CAP, LANES - 1)
         slot = jnp.bitwise_and(lane8 - first_lane, LANES - 1)
-        tile = jnp.zeros((16, LANES), F32)
+        tile = jnp.zeros((8, LANES), F32)
         for dc in range(2):
             owner = (jnp.right_shift(t, 4) * 2 + dc) * 16 + jnp.bitwise_and(t, 15)
             start = starts[owner]
             count = counts[0, owner]
-            send[i, dc * CAP : (dc + 1) * CAP, :] = rows_f32[pl.ds(start, CAP), :].astype(BF16)
+            rows = rows_f32[pl.ds(start, CAP), :].reshape(TILES, 8, LANES)
+            send[i, dc * TILES : (dc + 1) * TILES] = rows.astype(BF16)
             row = jnp.right_shift(start, 7)
             off = jnp.bitwise_and(start, LANES - 1)
             turn = jnp.bitwise_and(first_lane - off + LANES, LANES - 1)
@@ -113,15 +117,13 @@
             lat_row = jnp.where(valid, jnp.bitwise_and(jnp.right_shift(code, 7), 15), -1)
             lon_col = jnp.bitwise_and(code, 127)
             for k, part in enumerate((shift, lat_row, lon_col)):
-                part = part.astype(F32)
-                both = jnp.concatenate([part, part], axis=0)
-                tile = jnp.where(sub16 == dc * 3 + k, both, tile)
-        send[i, 2 * CAP : BLOCK, :] = tile.astype(BF16)
+                tile = jnp.where(sub8 == dc * 3 + k, part.astype(F32), tile)
+        send[i, 2 * TILES] = tile.astype(BF16)
 
     def block_copy(i):
         return pltpu.make_async_remote_copy(
             src_ref=send.at[i], dst_ref=recv.at[i], send_sem=send_sem,
-            recv_sem=recv_sem.at[jnp.right_shift(i, 4)], device_id=peer(i), device_id_type=MESH,
+            recv_sem=recv_sem.at[jnp.where(i < 48, jnp.right_shift(i, 4), jnp.right_shift(i, 3) - 3)], device_id=peer(i), device_id_type=MESH,
         )
 
     pack(0)
@@ -134,7 +136,7 @@
         block_copy(i).start()
         return carry
 
-    lax.fori_loop(1, CHIPS, post, 0, unroll=1)
+    lax.fori_loop(1, CHIPS, post, 0, unroll=3)
     for copy in loads[3:]:
         copy.wait()
 
@@ -156,7 +158,7 @@
         below = jnp.where(lev2 == 0, m, pltpu.roll(m, 1, 0))
         return m + d * (above - 2.0 * m + below)
 
-    def column_step(e, load):
+    def column_step(e, load, after_edges):
         def pair(j, packed):
             r0 = 2 * j
             f = jnp.concatenate([flx[pl.ds(r0, 1), :], flx[pl.ds(r0 + 1, 1), :]], axis=1)
@@ -172,7 +174,9 @@
                     packed = jnp.where((lane == at) | (lane == at + 1), turned, packed)
             return packed
 
-        return lax.fori_loop(0, CLAT // 2, pair, jnp.zeros((LEV, LANES), F32), unroll=8)
+        packed = pair(CLAT // 2 - 1, pair(0, jnp.zeros((LEV, LANES), F32)))
+        after_edges()
+        return lax.fori_loop(1, CLAT // 2 - 1, pair, packed, unroll=6)
 
     def halo_copies(e):
         def rc(src, dst, k, dev):
@@ -204,7 +208,7 @@
         we = jnp.where(lane == 0, turned, pltpu.roll(c, 1, 1))
         return c + g[0] * (ea - c) + g[1] * (c - we) + g[2] * (n - c) + g[3] * (c - s)
 
-    packed = column_step(0, lambda t, r: adj[pl.ds(t * LEV * CLAT + r, LEV, stride=CLAT), :])
+    packed = column_step(0, lambda t, r: adj[pl.ds(t * LEV * CLAT + r, LEV, stride=CLAT), :], lambda: None)
 
     def face_edge(r, packed):
         at = 64 + 2 * r
@@ -238,33 +242,36 @@
 
     row_id = iota((LANES, LANES), 0)
     eye = (row_id == iota((LANES, LANES), 1)).astype(F32).astype(BF16)
-    cells = iota((ROWS, 2 * LANES), 1).astype(F32)
-    clane = iota((16, LANES), 1)
+    clane = iota((8, LANES), 1)
 
     def place_group(blocks, tiles, fresh=False):
+        sources = blocks.shape[0]
+        count = sources * CAP
+        cells = iota((count, 2 * LANES), 1).astype(F32)
+        blocks = blocks.astype(F32).reshape(count, LANES).astype(BF16)
         parts = []
-        for h in range(GROUP // 8):
+        for h in range(sources // 8):
             s = [tiles[h * 8 + k].astype(F32) for k in range(8)]
             parts.append(jnp.where(clane < 48, s[0], jnp.where(clane < 96, s[1], s[2])))
             parts.append(
                 jnp.where(clane < 16, s[2], jnp.where(clane < 64, s[3], jnp.where(clane < 112, s[4], s[5])))
             )
             parts.append(jnp.where(clane < 32, s[5], jnp.where(clane < 80, s[6], s[7])))
-        codes[...] = jnp.concatenate(parts, axis=1)
-        shift = codes[pl.ds(core * 3, 1), :].astype(jnp.int32)
-        lat_row = codes[pl.ds(core * 3 + 1, 1), :]
-        lon_col = codes[pl.ds(core * 3 + 2, 1), :]
+        codes[:, :count] = jnp.concatenate(parts, axis=1)
+        shift = codes[pl.ds(core * 3, 1), :count].astype(jnp.int32)
+        lat_row = codes[pl.ds(core * 3 + 1, 1), :count]
+        lon_col = codes[pl.ds(core * 3 + 2, 1), :count]
         turned = lax.dot_general(eye, blocks, (((1,), (1,)), ((), ())), preferred_element_type=F32)
         placed = []
         for t in range(TR):
-            x = jnp.concatenate([turned[t * SPAN : (t + 1) * SPAN], jnp.zeros((8, ROWS), F32)], axis=0)
+            x = jnp.concatenate([turned[t * SPAN : (t + 1) * SPAN], jnp.zeros((8, count), F32)], axis=0)
             for bit in (1, 2, 4):
                 x = jnp.where(jnp.bitwise_and(shift, bit) != 0, pltpu.roll(x, bit, 0), x)
-            x8 = jnp.concatenate([jnp.zeros((8, ROWS), F32), x[: LEV - 8]], axis=0)
+            x8 = jnp.concatenate([jnp.zeros((8, count), F32), x[: LEV - 8]], axis=0)
             placed.append(jnp.where(jnp.bitwise_and(shift, 8) != 0, x8, x))
         placed = jnp.concatenate(placed, axis=0).astype(BF16)
         parity = jnp.bitwise_and(lat_row.astype(jnp.int32), 1).astype(F32)
-        cell = jnp.broadcast_to(parity * LANES + lon_col, (8, ROWS))
+        cell = jnp.broadcast_to(parity * LANES + lon_col, (8, count))
         hot = jnp.where(jnp.transpose(cell)[:, 0:1] == cells, 1.0, 0.0).astype(BF16)
         for j in range(CLAT // 2):
             mine = jnp.where((lat_row == 2 * j) | (lat_row == 2 * j + 1), 1.0, 0.0).astype(BF16)
@@ -276,40 +283,40 @@
                 acc[2 * j] += res[:, :LANES]
                 acc[2 * j + 1] += res[:, LANES:]
 
-    mine_at = pl.ds(pl.multiple_of(core * CAP, 16), CAP)
-    other_at = pl.ds(pl.multiple_of(CAP - core * CAP, 16), CAP)
+    mine_at = pl.ds(core * TILES, TILES)
+    other_at = pl.ds(TILES - core * TILES, TILES)
 
     def forwards(g):
-        at = pl.ds(g * GROUP, GROUP)
+        at = pl.ds(*GROUPS[g])
         return [
             pltpu.make_async_remote_copy(
-                src_ref=recv.at[at, other_at, :], dst_ref=fwd.at[at],
+                src_ref=recv.at[at, other_at], dst_ref=fwd.at[at],
                 send_sem=fwd_send.at[0, g], recv_sem=fwd_recv.at[0, g],
                 device_id=(sibling, lon), device_id_type=MESH,
             ),
             pltpu.make_async_remote_copy(
-                src_ref=recv.at[at, 2 * CAP : BLOCK, :], dst_ref=fwdc.at[at],
+                src_ref=recv.at[at, 2 * TILES], dst_ref=fwdc.at[at],
                 send_sem=fwd_send.at[1, g], recv_sem=fwd_recv.at[1, g],
                 device_id=(sibling, lon), device_id_type=MESH,
             ),
         ]
 
     def arrived(g, lo):
-        at = pl.ds(g * GROUP + lo, GROUP - lo)
+        at = pl.ds(GROUPS[g][0] + lo, GROUPS[g][1] - lo)
         pltpu.make_async_remote_copy(
             src_ref=send.at[at], dst_ref=recv.at[at], send_sem=send_sem,
             recv_sem=recv_sem.at[g], device_id=(sibling, lon), device_id_type=MESH,
         ).wait_recv()
 
     def place_direct(g):
-        at = pl.ds(g * GROUP, GROUP)
-        place_group(recv[at, mine_at, :].reshape(ROWS, LANES), recv[at, 2 * CAP : BLOCK, :], g == 0)
+        at = pl.ds(*GROUPS[g])
+        place_group(recv[at, mine_at], recv[at, 2 * TILES], g == 0)
 
     def place_forwarded(g):
         for copy in forwards(g):
             copy.wait_recv()
-        at = pl.ds(g * GROUP, GROUP)
-        place_group(fwd[at].reshape(ROWS, LANES), fwdc[at])
+        at = pl.ds(*GROUPS[g])
+        place_group(fwd[at], fwdc[at])
 
     own.wait()
 
@@ -331,12 +338,19 @@
     place_forwarded(1)
     place_forwarded(2)
     take(3)
+    take(4)
+    place_forwarded(3)
     finish_first()
-    place_forwarded(3)
-
-    edges[1] = column_step(1, lambda t, r: acc[r, t * LEV : (t + 1) * LEV, :])
+    place_forwarded(4)
+
     second_halo = halo_copies(1)
-    for copy in second_halo:
+
+    def planes():
+        for copy in second_halo[2:]:
+            copy.start()
+
+    edges[1] = column_step(1, lambda t, r: acc[r, t * LEV : (t + 1) * LEV, :], planes)
+    for copy in second_halo[:2]:
         copy.start()
     for copy in second_halo:
         copy.wait()
@@ -351,7 +365,7 @@
         return carry
 
     lax.fori_loop(0, CLAT, second_row, 0, unroll=4)
-    for g in range(GROUPS):
+    for g in range(len(GROUPS)):
         for copy in forwards(g):
             copy.wait_send()
     every = pl.ds(1, CHIPS - 1)
@@ -359,6 +373,23 @@
         src_ref=send.at[every], dst_ref=recv.at[every], send_sem=send_sem,
         recv_sem=recv_sem.at[0], device_id=(sibling, lon), device_id_type=MESH,
     ).wait_send()
+
+
+def finish_kernel(out_in, flux_in, out, flux, held, held_flux, sems):
+    rows = TR * LEV * CLAT // COPIES
+    parts = [(out_in, held, out, pl.ds(k * rows, rows)) for k in range(COPIES)]
+    parts.append((flux_in, held_flux, flux, pl.ds(0, TR * CLAT)))
+    loads, stores = [], []
+    for k, (src, mid, dst, at) in enumerate(parts):
+        loads.append(pltpu.make_async_copy(src.at[at], mid.at[at], sems.at[0, k]))
+        stores.append(pltpu.make_async_copy(mid.at[at], dst.at[at], sems.at[1, k]))
+    for copy in loads:
+        copy.start()
+    for load, store in zip(loads, stores):
+        load.wait()
+        store.start()
+    for copy in stores:
+        copy.wait()
 
 
 def local(adjoint_state, courant_east, courant_north, diffusion, convective_flux, convection,
@@ -388,24 +419,24 @@
             pltpu.VMEM((56, LANES), jnp.int32),
             pltpu.SMEM((128,), jnp.int32),
             dma((9,)),
-            pltpu.VMEM((CHIPS, BLOCK, LANES), BF16),
-            pltpu.VMEM((CHIPS, BLOCK, LANES), BF16),
-            pltpu.VMEM((CHIPS, CAP, LANES), BF16),
-            pltpu.VMEM((CHIPS, 16, LANES), BF16),
+            pltpu.VMEM((CHIPS, BLOCK, 8, LANES), BF16),
+            pltpu.VMEM((CHIPS, BLOCK, 8, LANES), BF16),
+            pltpu.VMEM((CHIPS, TILES, 8, LANES), BF16),
+            pltpu.VMEM((CHIPS, 8, LANES), BF16),
             pltpu.VMEM((CLAT, TR * LEV, LANES), F32),
             pltpu.VMEM((2, CLAT + 2, TR * LEV, LANES), F32),
             pltpu.VMEM((4, CLAT, LEV, LANES), F32),
             pltpu.VMEM((256, LANES), F32),
-            pltpu.VMEM((16, ROWS), F32),
+            pltpu.VMEM((8, 16 * CAP), F32),
             pltpu.VMEM((2, LEV, LANES), F32),
             pltpu.VMEM((2, LEV, LANES), F32),
             pltpu.VMEM((2, LEV, LANES), F32),
             pltpu.VMEM((LEV, LANES), F32),
             pltpu.VMEM((LEV, LANES), F32),
             dma,
-            dma((GROUPS,)),
-            dma((2, GROUPS)),
-            dma((2, GROUPS)),
+            dma((len(GROUPS),)),
+            dma((2, len(GROUPS))),
+            dma((2, len(GROUPS))),
             dma((2, 5)),
             dma((2, 5)),
             dma,
@@ -424,6 +455,23 @@
         sounding_column.reshape(listed // LANES, LANES),
         sounding_level.reshape(listed // LANES, LANES),
     )
+    anywhere = pl.BlockSpec(memory_space=pl.ANY)
+    out, flux = pl.pallas_call(
+        finish_kernel,
+        out_shape=(
+            jax.ShapeDtypeStruct((TR * LEV * CLAT, LANES), F32),
+            jax.ShapeDtypeStruct((TR * CLAT, LANES), F32),
+        ),
+        in_specs=[anywhere] * 2,
+        out_specs=(anywhere, anywhere),
+        scratch_shapes=[
+            pltpu.VMEM((TR * LEV * CLAT, LANES), F32),
+            pltpu.VMEM((TR * CLAT, LANES), F32),
+            dma((2, COPIES + 1)),
+        ],
+        compiler_params=pltpu.CompilerParams(vmem_limit_bytes=60 << 20),
+        name="finish",
+    )(out, flux)
     return out.reshape(TR, LEV, CLAT, LANES), flux.reshape(TR, CLAT, LANES)
 
 

time: 50.3 us -> 49.2 us (0.978)
  local copies, waits for them, and re-layouts: 2.97 us -> 0 us
  Pallas kernels: 46.5 us -> 48.1 us
    unnamed x4 -> x0, local copies, waits for them, and re-layouts: 2.97 us -> none
    pallas_call x0 -> x1, Pallas kernels: none -> 2.06 us  [local(): pl.pallas_call(finish_kernel, out_shape=(jax.ShapeDtypeStruct((TR * LEV *...]
where the time goes in v4:
time: 49.2 us; the launch traced here: 48.8 us
  Pallas kernels  48.1 us (98%)
  between operations  0.64 us (1%)
    pallas_call x1, Pallas kernels, local(): pl.pallas_call(main_kernel, out_shape=(jax.ShapeDtypeStruct((TR * LEV * C...  46.1 us
    pallas_call x1, Pallas kernels, local(): pl.pallas_call(finish_kernel, out_shape=(jax.ShapeDtypeStruct((TR * LEV *...  2.06 us

profile of v4, /device:TPU:0, one launch (start us, length us, event | category | flops | bytes accessed | tf_op | source)
XLA Modules:
  0.0 48.8 jit_solution(7844598067878053774)
XLA Ops:
  0.6 46.1 %transport.1 = (f32[2304,128]{1,0:T(8,128)}, f32[32,128]{1,0:T(8,128)}) custom-call(s32[1,128]{1,0:T(1,128)} %counts.1, f32[2304,128]{1,0:T(8,128)} %bitcast.7, f32[1152,128]{1,0:T(8,128)} %bitcast.8, f32[1152,128]{1,0:T(8,128)} %bitcast.9, f32[16,128]{1,0:T(8,128)} %dif_hbm.1, f32[16,128]{1,0:T(8,128)} %flx_hbm.1, f32[72,72]{1,0:T(8,128)} %conv_hbm.1, ...), custom_call_target="tpu_custom_call" | custom-call | tf_op jit(solution)/shard_map/transport/pallas_call | solution.py:400
  46.7 2.1 %finish.1 = (f32[2304,128]{1,0:T(8,128)}, f32[32,128]{1,0:T(8,128)}) custom-call(f32[2304,128]{1,0:T(8,128)} %get-tuple-element.6.out_in, f32[32,128]{1,0:T(8,128)} %get-tuple-element.7.flux_in), custom_call_target="tpu_custom_call" | custom-call | tf_op jit(solution)/shard_map/finish/pallas_call | solution.py:459

commit v5 on v4

--- a/solution.py
+++ b/solution.py
@@ -12,7 +12,7 @@
 CLAT = 16
 LANES = 128
 CHIPS = 64
-STRIDE = 45
+STRIDE = 27
 TILES = CAP // 8
 BLOCK = 2 * TILES + 1
 GROUPS = ((0, 16), (16, 16), (32, 16), (48, 8), (56, 8))
@@ -38,10 +38,11 @@
 
 def main_kernel(
     counts, adj_hbm, ce_hbm, cn_hbm, dif_hbm, flx_hbm, conv_hbm, forcing_hbm, column_hbm, level_hbm,
-    out, flux,
+    out_hbm, flux_hbm,
+    out, flux, out_sem,
     adj, ce, cn, dif, flx, conv, forcing, column, level,
     rows_f32, targets, starts, load_sem,
-    send, recv, fwd, fwdc, acc, field, gains, mixer, codes, edges, west_in, east_in, cn_edge, cn_south,
+    send, recv, fwd, acc, field, gains, mixer, codes, edges, west_in, east_in, cn_edge, cn_south,
     send_sem, recv_sem, fwd_send, fwd_recv, halo_send, halo_recv, self_sem,
 ):
     lat, lon, core, chip = place()
@@ -105,7 +106,8 @@
             start = starts[owner]
             count = counts[0, owner]
             rows = rows_f32[pl.ds(start, CAP), :].reshape(TILES, 8, LANES)
-            send[i, dc * TILES : (dc + 1) * TILES] = rows.astype(BF16)
+            at = dc * (TILES + 1)
+            send[i, at : at + TILES] = rows.astype(BF16)
             row = jnp.right_shift(start, 7)
             off = jnp.bitwise_and(start, LANES - 1)
             turn = jnp.bitwise_and(first_lane - off + LANES, LANES - 1)
@@ -118,7 +120,7 @@
             lon_col = jnp.bitwise_and(code, 127)
             for k, part in enumerate((shift, lat_row, lon_col)):
                 tile = jnp.where(sub8 == dc * 3 + k, part.astype(F32), tile)
-        send[i, 2 * TILES] = tile.astype(BF16)
+        send[i, TILES] = tile.astype(BF16)
 
     def block_copy(i):
         return pltpu.make_async_remote_copy(
@@ -283,22 +285,17 @@
                 acc[2 * j] += res[:, :LANES]
                 acc[2 * j + 1] += res[:, LANES:]
 
-    mine_at = pl.ds(core * TILES, TILES)
-    other_at = pl.ds(TILES - core * TILES, TILES)
+    mine_at = pl.ds(core * (TILES + 1), TILES)
+    other_at = pl.ds(TILES - core * TILES, TILES + 1)
 
     def forwards(g):
         at = pl.ds(*GROUPS[g])
         return [
             pltpu.make_async_remote_copy(
                 src_ref=recv.at[at, other_at], dst_ref=fwd.at[at],
-                send_sem=fwd_send.at[0, g], recv_sem=fwd_recv.at[0, g],
+                send_sem=fwd_send.at[g], recv_sem=fwd_recv.at[g],
                 device_id=(sibling, lon), device_id_type=MESH,
-            ),
-            pltpu.make_async_remote_copy(
-                src_ref=recv.at[at, 2 * TILES], dst_ref=fwdc.at[at],
-                send_sem=fwd_send.at[1, g], recv_sem=fwd_recv.at[1, g],
-                device_id=(sibling, lon), device_id_type=MESH,
-            ),
+            )
         ]
 
     def arrived(g, lo):
@@ -310,13 +307,13 @@
 
     def place_direct(g):
         at = pl.ds(*GROUPS[g])
-        place_group(recv[at, mine_at], recv[at, 2 * TILES], g == 0)
+        place_group(recv[at, mine_at], recv[at, TILES], g == 0)
 
     def place_forwarded(g):
         for copy in forwards(g):
             copy.wait_recv()
         at = pl.ds(*GROUPS[g])
-        place_group(fwd[at], fwdc[at])
+        place_group(fwd[at, pl.ds(core, TILES)], fwd[at, TILES - core * TILES])
 
     own.wait()
 
@@ -352,19 +349,48 @@
     edges[1] = column_step(1, lambda t, r: acc[r, t * LEV : (t + 1) * LEV, :], planes)
     for copy in second_halo[:2]:
         copy.start()
+    def inner_row(r, carry):
+        g = tuple(gains[k, r] for k in range(4))
+        for t in range(TR):
+            rows = pl.ds(t * LEV, LEV)
+            c = field[1, r + 1, rows, :]
+            n = field[1, r + 2, rows, :]
+            s = field[1, r, rows, :]
+            ea = jnp.where(lane == LANES - 1, 0.0, pltpu.roll(c, LANES - 1, 1))
+            we = jnp.where(lane == 0, 0.0, pltpu.roll(c, 1, 1))
+            out[pl.ds(t * LEV * CLAT + r, LEV, stride=CLAT), :] = (
+                c + g[0] * (ea - c) + g[1] * (c - we) + g[2] * (n - c) + g[3] * (c - s)
+            )
+        return carry
+
+    lax.fori_loop(1, CLAT - 1, inner_row, 0, unroll=7)
     for copy in second_halo:
         copy.wait()
     halo1 = merged(1)
-
-    def second_row(r, carry):
-        g = tuple(gains[k, r] for k in range(4))
-        for t in range(TR):
-            y = advected(1, r, t, halo1, g)
+    side = jnp.where(lane == LANES - 1, 1.0, 0.0)
+    stores = []
+    for t in range(TR):
+
+        def finished(r, y, t=t):
             out[pl.ds(t * LEV * CLAT + r, LEV, stride=CLAT), :] = y
             flux[pl.ds(t * CLAT + r, 1), :] = y[0:1] + acc[r, t * LEV : t * LEV + 1, :]
-        return carry
-
-    lax.fori_loop(0, CLAT, second_row, 0, unroll=4)
+
+        def outer_row(r, carry, t=t, finished=finished):
+            at = 2 * (t * CLAT + r)
+            turned = pltpu.roll(halo1, lax.rem(2 * LANES - at, LANES), 1)
+            y = out[pl.ds(t * LEV * CLAT + r, LEV, stride=CLAT), :]
+            finished(r, y + turned * jnp.where(lane == 0, -gains[1, r], side * gains[0, r]))
+            return carry
+
+        lax.fori_loop(1, CLAT - 1, outer_row, 0, unroll=7)
+        for r in (0, CLAT - 1):
+            g = tuple(gains[k, r] for k in range(4))
+            finished(r, advected(1, r, t, halo1, g))
+        at = pl.ds(t * LEV * CLAT, LEV * CLAT)
+        stores.append(pltpu.make_async_copy(out.at[at], out_hbm.at[at], out_sem.at[t]))
+        stores[-1].start()
+    stores.append(pltpu.make_async_copy(flux, flux_hbm, out_sem.at[TR]))
+    stores[-1].start()
     for g in range(len(GROUPS)):
         for copy in forwards(g):
             copy.wait_send()
@@ -373,6 +399,8 @@
         src_ref=send.at[every], dst_ref=recv.at[every], send_sem=send_sem,
         recv_sem=recv_sem.at[0], device_id=(sibling, lon), device_id_type=MESH,
     ).wait_send()
+    for copy in stores:
+        copy.wait()
 
 
 def finish_kernel(out_in, flux_in, out, flux, held, held_flux, sems):
@@ -394,7 +422,6 @@
 
 def local(adjoint_state, courant_east, courant_north, diffusion, convective_flux, convection,
           sounding_forcing, sounding_column, sounding_level, owner_counts):
-    vmem = pl.BlockSpec(memory_space=pltpu.VMEM)
     dma = pltpu.SemaphoreType.DMA
     listed = sounding_forcing.shape[0]
     out, flux = pl.pallas_call(
@@ -404,8 +431,11 @@
             jax.ShapeDtypeStruct((TR * CLAT, LANES), F32),
         ),
         in_specs=[pl.BlockSpec(memory_space=pltpu.SMEM)] + [pl.BlockSpec(memory_space=pl.ANY)] * 9,
-        out_specs=(vmem, vmem),
+        out_specs=(pl.BlockSpec(memory_space=pl.ANY), pl.BlockSpec(memory_space=pl.ANY)),
         scratch_shapes=[
+            pltpu.VMEM((TR * LEV * CLAT, LANES), F32),
+            pltpu.VMEM((TR * CLAT, LANES), F32),
+            dma((TR + 1,)),
             pltpu.VMEM((TR * LEV * CLAT, LANES), F32),
             pltpu.VMEM((LEV * CLAT, LANES), F32),
             pltpu.VMEM((LEV * CLAT, LANES), F32),
@@ -421,8 +451,7 @@
             dma((9,)),
             pltpu.VMEM((CHIPS, BLOCK, 8, LANES), BF16),
             pltpu.VMEM((CHIPS, BLOCK, 8, LANES), BF16),
-            pltpu.VMEM((CHIPS, TILES, 8, LANES), BF16),
-            pltpu.VMEM((CHIPS, 8, LANES), BF16),
+            pltpu.VMEM((CHIPS, TILES + 1, 8, LANES), BF16),
             pltpu.VMEM((CLAT, TR * LEV, LANES), F32),
             pltpu.VMEM((2, CLAT + 2, TR * LEV, LANES), F32),
             pltpu.VMEM((4, CLAT, LEV, LANES), F32),
@@ -435,8 +464,8 @@
             pltpu.VMEM((LEV, LANES), F32),
             dma,
             dma((len(GROUPS),)),
-            dma((2, len(GROUPS))),
-            dma((2, len(GROUPS))),
+            dma((len(GROUPS),)),
+            dma((len(GROUPS),)),
             dma((2, 5)),
             dma((2, 5)),
             dma,

time: 49.2 us -> 48.7 us (0.990)
  Pallas kernels: 48.1 us -> 47.6 us
    pallas_call x1, Pallas kernels: 46.1 us -> 45.6 us  [local(): pl.pallas_call(main_kernel, out_shape=(jax.ShapeDtypeStruct((TR * LEV * C...]
where the time goes in v5:
time: 48.7 us; the launch traced here: 48.3 us
  Pallas kernels  47.6 us (98%)
  between operations  0.64 us (1%)
    pallas_call x1, Pallas kernels, local(): pl.pallas_call(main_kernel, out_shape=(jax.ShapeDtypeStruct((TR * LEV * C...  45.6 us
    pallas_call x1, Pallas kernels, local(): pl.pallas_call(finish_kernel, out_shape=(jax.ShapeDtypeStruct((TR * LEV *...  2.06 us

profile of v5, /device:TPU:0, one launch (start us, length us, event | category | flops | bytes accessed | tf_op | source)
XLA Modules:
  0.0 48.3 jit_solution(15351391607682004127)
XLA Ops:
  0.6 45.6 %transport.1 = (f32[2304,128]{1,0:T(8,128)}, f32[32,128]{1,0:T(8,128)}) custom-call(s32[1,128]{1,0:T(1,128)} %counts.1, f32[2304,128]{1,0:T(8,128)} %bitcast.7, f32[1152,128]{1,0:T(8,128)} %bitcast.8, f32[1152,128]{1,0:T(8,128)} %bitcast.9, f32[16,128]{1,0:T(8,128)} %dif_hbm.1, f32[16,128]{1,0:T(8,128)} %flx_hbm.1, f32[72,72]{1,0:T(8,128)} %conv_hbm.1, ...), custom_call_target="tpu_custom_call" | custom-call | tf_op jit(solution)/shard_map/transport/pallas_call | solution.py:427
  46.2 2.1 %finish.1 = (f32[2304,128]{1,0:T(8,128)}, f32[32,128]{1,0:T(8,128)}) custom-call(f32[2304,128]{1,0:T(8,128)} %get-tuple-element.6.out_in, f32[32,128]{1,0:T(8,128)} %get-tuple-element.7.flux_in), custom_call_target="tpu_custom_call" | custom-call | tf_op jit(solution)/shard_map/finish/pallas_call | solution.py:488

commit v6 on v5

--- a/solution.py
+++ b/solution.py
@@ -129,16 +129,18 @@
         )
 
     pack(0)
+    pack(1)
     own = pltpu.make_async_copy(send.at[0], recv.at[0], self_sem)
     own.start()
     pl.semaphore_wait(barrier, CHIPS + 1)
 
     def post(i, carry):
-        pack(i)
         block_copy(i).start()
+        pack(i + 1)
         return carry
 
-    lax.fori_loop(1, CHIPS, post, 0, unroll=3)
+    lax.fori_loop(1, CHIPS - 1, post, 0, unroll=2)
+    block_copy(CHIPS - 1).start()
     for copy in loads[3:]:
         copy.wait()
 

time: 48.7 us -> 48.6 us (level)
  no operation moved by 1% of the time
where the time goes in v6:
time: 48.6 us; the launch traced here: 48.2 us
  Pallas kernels  47.5 us (98%)
  between operations  0.64 us (1%)
    pallas_call x1, Pallas kernels, local(): pl.pallas_call(main_kernel, out_shape=(jax.ShapeDtypeStruct((TR * LEV * C...  45.5 us
    pallas_call x1, Pallas kernels, local(): pl.pallas_call(finish_kernel, out_shape=(jax.ShapeDtypeStruct((TR * LEV *...  2.06 us

profile of v6, /device:TPU:0, one launch (start us, length us, event | category | flops | bytes accessed | tf_op | source)
XLA Modules:
  0.0 48.2 jit_solution(9236212585395593362)
XLA Ops:
  0.6 45.5 %transport.1 = (f32[2304,128]{1,0:T(8,128)}, f32[32,128]{1,0:T(8,128)}) custom-call(s32[1,128]{1,0:T(1,128)} %counts.1, f32[2304,128]{1,0:T(8,128)} %bitcast.7, f32[1152,128]{1,0:T(8,128)} %bitcast.8, f32[1152,128]{1,0:T(8,128)} %bitcast.9, f32[16,128]{1,0:T(8,128)} %dif_hbm.1, f32[16,128]{1,0:T(8,128)} %flx_hbm.1, f32[72,72]{1,0:T(8,128)} %conv_hbm.1, ...), custom_call_target="tpu_custom_call" | custom-call | tf_op jit(solution)/shard_map/transport/pallas_call | solution.py:429
  46.1 2.1 %finish.1 = (f32[2304,128]{1,0:T(8,128)}, f32[32,128]{1,0:T(8,128)}) custom-call(f32[2304,128]{1,0:T(8,128)} %get-tuple-element.6.out_in, f32[32,128]{1,0:T(8,128)} %get-tuple-element.7.flux_in), custom_call_target="tpu_custom_call" | custom-call | tf_op jit(solution)/shard_map/finish/pallas_call | solution.py:490
